TPU v7x, 128 devices: a whole 4x4x4 slice. The times are simulated.
128 devices in a mesh: row: 8 (over y, z_lo), col: 16 (over x, z_hi, core).
Axes of the slice: x: 4, y: 4, z: 4 (z_hi: 2, z_lo: 2; z = z_hi * 2 + z_lo), core: 2. Of those that a mesh axis runs over, the one named last changes fastest.
Arguments:
- pair_state: bfloat16 [384, 384, 128], P('row', 'col'), may hold values from -6 to 6
- tile_mask: int32 [3, 3], replicated, may hold values from 0 to 1, as said below
- weight_in: bfloat16 [2, 128, 640], replicated, may hold values from -0.5 to 0.5
- weight_out: bfloat16 [2, 128, 128], replicated, may hold values from -0.5 to 0.5
- gain_in: float32 [2, 128], replicated, may hold values from 0.1 to 1.9
- gain_out: float32 [2, 128], replicated, may hold values from 0.1 to 1.9
- cotangent: bfloat16 [384, 384, 128], P('row', 'col'), may hold values from -6 to 6
Outputs:
- updated_pair: bfloat16 [384, 384, 128], P('row', 'col')
- pair_grad: float32 [384, 384, 128], P('row', 'col')
Inputs may be any that keep to these rules, and one draw needn't show every extreme that they name: `tile_mask`: Symmetric. The tiles form runs of consecutive chains, at least two; every tile pair inside one chain is 1, and all tile pairs of one pair of chains share one value.
All inputs are finite; a program needn't handle non-finite values.
Results may differ from a plain program's by a relative error of at most 0.012.
Values may be sent and summed in bfloat16 or wider, within the bound.
No kernel may reach another device: no remote copies, remote signals or barrier semaphores. Data moves between devices by JAX's collectives and lax.ppermute only.
A program may use at most 128 MiB of HBM per device.

v0:
```python
import jax
import jax.numpy as jnp
from jax import lax
from jax.sharding import PartitionSpec as P

RES = 384
TILES = 3


norm_eps = 1e-05


def normalize(values):
    center = values - jnp.mean(values, axis=-1, keepdims=True)
    inv_scale = lax.rsqrt(jnp.mean(center * center, axis=-1, keepdims=True) + norm_eps)
    return (center * inv_scale, inv_scale)


def norm_back(standard, inv_scale, gain_vec, upstream):
    scaled = upstream * gain_vec
    return inv_scale * (
        scaled
        - jnp.mean(scaled, axis=-1, keepdims=True)
        - standard * jnp.mean(scaled * standard, axis=-1, keepdims=True)
    )


def project(pair_in, tile_gate, weight_layer, gain_vec):
    standard, inv_scale = normalize(pair_in.astype(jnp.float32))
    normed = (standard * gain_vec).astype(jnp.bfloat16)
    channels = pair_in.shape[-1]
    hidden = (weight_layer.shape[1] - channels) // 4
    projected = jnp.dot(
        normed.reshape(-1, channels), weight_layer, preferred_element_type=jnp.float32
    )
    projected = projected.reshape(pair_in.shape[:-1] + (weight_layer.shape[1],))
    gate_col = tile_gate[..., None]
    left_side = (
        gate_col * jax.nn.sigmoid(projected[..., hidden : 2 * hidden]) * projected[..., :hidden]
    ).astype(jnp.bfloat16)
    right_side = (
        gate_col
        * jax.nn.sigmoid(projected[..., 3 * hidden : 4 * hidden])
        * projected[..., 2 * hidden : 3 * hidden]
    ).astype(jnp.bfloat16)
    return (standard, inv_scale, projected, left_side, right_side)


def finish(pair_in, inner_sum, projected, tile_gate, weight_layer, gain_vec):
    standard, inv_scale = normalize(inner_sum)
    normed = (standard * gain_vec).astype(jnp.bfloat16)
    hidden = inner_sum.shape[-1]
    update = jnp.dot(
        normed.reshape(-1, hidden), weight_layer, preferred_element_type=jnp.float32
    ).reshape(pair_in.shape)
    gate_sig = jax.nn.sigmoid(projected[..., 4 * hidden :])
    result = (pair_in.astype(jnp.float32) + tile_gate[..., None] * gate_sig * update).astype(
        jnp.bfloat16
    )
    return (result, (standard, inv_scale, update))


def back_top(upstream, projected, tile_gate, saved, weight_layer, gain_vec):
    standard, inv_scale, update = saved
    hidden = weight_layer.shape[0]
    channels = weight_layer.shape[1]
    gate_sig = jax.nn.sigmoid(projected[..., 4 * hidden :])
    gated_grad = upstream * tile_gate[..., None]
    d_update = (gated_grad * gate_sig).astype(jnp.bfloat16)
    d_outgate = gated_grad * update * gate_sig * (1.0 - gate_sig)
    d_normed = jnp.dot(
        d_update.reshape(-1, channels), weight_layer.T, preferred_element_type=jnp.float32
    ).reshape(standard.shape)
    d_inner = norm_back(standard, inv_scale, gain_vec, d_normed).astype(jnp.bfloat16)
    return (d_inner, d_outgate)


def back_bottom(
    upstream,
    d_left,
    d_right,
    d_outgate,
    projected,
    tile_gate,
    standard,
    inv_scale,
    weight_layer,
    gain_vec,
):
    hidden = d_left.shape[-1]
    gate_col = tile_gate[..., None]
    left_sig = jax.nn.sigmoid(projected[..., hidden : 2 * hidden])
    right_sig = jax.nn.sigmoid(projected[..., 3 * hidden : 4 * hidden])
    pieces = [
        d_left * gate_col * left_sig,
        d_left * gate_col * projected[..., :hidden] * left_sig * (1.0 - left_sig),
        d_right * gate_col * right_sig,
        d_right
        * gate_col
        * projected[..., 2 * hidden : 3 * hidden]
        * right_sig
        * (1.0 - right_sig),
        d_outgate,
    ]
    d_proj = jnp.concatenate(pieces, axis=-1).astype(jnp.bfloat16)
    d_normed = jnp.dot(
        d_proj.reshape(-1, d_proj.shape[-1]), weight_layer.T, preferred_element_type=jnp.float32
    ).reshape(standard.shape)
    return upstream + norm_back(standard, inv_scale, gain_vec, d_normed)


def gather_rows(block):
    return lax.all_gather(block, "row", axis=0, tiled=True)


def gather_cols(block):
    return lax.all_gather(block, "col", axis=1, tiled=True)


def sum_cols(term_fn, row_total):
    return lax.psum_scatter(
        term_fn(jnp.int32(0), row_total * lax.axis_size("col")),
        "col",
        scatter_dimension=0,
        tiled=True,
    )


def sum_rows(term_fn, row_total):
    return lax.psum_scatter(
        term_fn(jnp.int32(0), row_total * lax.axis_size("row")),
        "row",
        scatter_dimension=0,
        tiled=True,
    )


def body(pair_state, tile_mask, weight_in, weight_out, gain_in, gain_out, cotangent):
    row_count = pair_state.shape[0]
    col_count = pair_state.shape[1]
    tile_width = RES // TILES
    row_first = lax.axis_index("row") * row_count
    col_first = lax.axis_index("col") * col_count
    tile_range = jnp.arange(TILES, dtype=jnp.int32)
    row_tiles = (row_first + jnp.arange(row_count, dtype=jnp.int32)) // tile_width
    col_tiles = (col_first + jnp.arange(col_count, dtype=jnp.int32)) // tile_width
    row_onehot = (row_tiles[:, None] == tile_range[None, :]).astype(jnp.float32)
    col_onehot = (col_tiles[:, None] == tile_range[None, :]).astype(jnp.float32)
    tile_gate = jnp.dot(
        jnp.dot(row_onehot, tile_mask.astype(jnp.float32), precision=lax.Precision.HIGHEST),
        col_onehot.T,
        precision=lax.Precision.HIGHEST,
    )
    front = project(pair_state, tile_gate, weight_in[0], gain_in[0])
    left_front = front[3]
    right_front = front[4]
    right_every = gather_rows(right_front)

    def front_terms(begin_at, take_rows):
        return jnp.einsum(
            "jkh,ikh->jih", right_every, left_front, preferred_element_type=jnp.float32
        )

    inner_front = jnp.transpose(sum_cols(front_terms, col_count), (1, 0, 2))
    middle_pair, top_front = finish(
        pair_state, inner_front, front[2], tile_gate, weight_out[0], gain_out[0]
    )
    second = project(middle_pair, tile_gate, weight_in[1], gain_in[1])
    left_second = second[3]
    right_second = second[4]
    left_rows_second = gather_cols(left_second)

    def second_terms(begin_at, take_rows):
        return jnp.einsum(
            "kih,kjh->ijh", left_rows_second, right_second, preferred_element_type=jnp.float32
        )

    inner_second = sum_rows(second_terms, row_count)
    updated_pair, top_second = finish(
        middle_pair, inner_second, second[2], tile_gate, weight_out[1], gain_out[1]
    )
    grad_last = cotangent.astype(jnp.float32)
    d_inner_second, d_gate_second = back_top(
        grad_last, second[2], tile_gate, top_second, weight_out[1], gain_out[1]
    )
    grad_cols = gather_rows(d_inner_second)
    d_right_second = jnp.einsum(
        "kih,ijh->kjh", left_rows_second, grad_cols, preferred_element_type=jnp.float32
    )

    def second_back_terms(begin_at, take_rows):
        return jnp.einsum(
            "ijh,kjh->ikh", grad_cols, right_second, preferred_element_type=jnp.float32
        )

    d_left_second = jnp.transpose(sum_cols(second_back_terms, col_count), (1, 0, 2))
    grad_middle = back_bottom(
        grad_last,
        d_left_second,
        d_right_second,
        d_gate_second,
        second[2],
        tile_gate,
        second[0],
        second[1],
        weight_in[1],
        gain_in[1],
    )
    d_inner_front, d_gate_front = back_top(
        grad_middle, front[2], tile_gate, top_front, weight_out[0], gain_out[0]
    )
    grad_rows = gather_cols(d_inner_front)
    d_left_front = jnp.einsum(
        "ijh,jkh->ikh", grad_rows, right_every, preferred_element_type=jnp.float32
    )

    def front_back_terms(begin_at, take_rows):
        return jnp.einsum("ijh,ikh->jkh", grad_rows, left_front, preferred_element_type=jnp.float32)

    d_right_front = sum_rows(front_back_terms, row_count)
    pair_grad = back_bottom(
        grad_middle,
        d_left_front,
        d_right_front,
        d_gate_front,
        front[2],
        tile_gate,
        front[0],
        front[1],
        weight_in[0],
        gain_in[0],
    )
    return (updated_pair, pair_grad)


def solution(mesh):
    return jax.shard_map(
        body,
        mesh=mesh,
        in_specs=(P("row", "col", None), P(), P(), P(), P(), P(), P("row", "col", None)),
        out_specs=(P("row", "col", None), P("row", "col", None)),
        check_vma=False,
    )
```

profile of v0, /device:TPU:1, one launch (start us, length us, event | category | flops | bytes accessed | tf_op | source)
XLA Modules:
  0.0 826.5 jit_solution(8144112895082879412)
XLA Ops:
  8.0 1.2 convert_reduce_fusion.1
  9.2 1.4 fusion.22
  11.8 1.8 fusion.61
  13.7 1.7 copy-done
  17.0 57.6 %all-gather.5.cloned.1.call-done = bf16[384,24,128]{2,1,0:T(8,128)(2,1)} async-done(((bf16[48,24,128]{2,1,0:T(8,128)(2,1)}), bf16[384,24,128]{2,1,0:T(8,128)(2,1)}) %all-gather.5.cloned.1.call-update) | async-done | bytes 2359312 | tf_op jit(solution)/shard_map/all_gather | solution.py:113
  74.6 3.7 copy.75
  78.3 5.1 convolution_bitcast_fusion
  83.4 9.8 %copy.76 = f32[384,48,128]{2,1,0:T(8,128)} copy(f32[384,48,128]{0,1,2:T(8,128)} %convolution_bitcast_fusion) | data formatting | bytes 18874368 | tf_op jit(solution)/shard_map/jkh,ikh->jih/transpose | solution.py:160
  93.9 107.4 %reduce-scatter.5.cloned.1.call-done = f32[24,48,128]{2,1,0:T(8,128)} async-done(((f32[384,48,128]{2,1,0:T(8,128)}), f32[24,48,128]{2,1,0:T(8,128)}) %reduce-scatter.5.cloned.1.call-update) | async-done | bytes 589840 | tf_op jit(solution)/shard_map/reduce_scatter | solution.py:121
  201.2 1.3 bitcast_reduce_fusion
  202.6 1.5 multiply_reduce_fusion.3
  204.1 2.7 convert_reduce_fusion
  208.4 1.5 copy-done.2
  211.2 1.4 copy.78
  212.6 59.9 %all-gather.7.cloned.1.call-done = bf16[48,384,128]{2,1,0:T(8,128)(2,1)} async-done(((bf16[48,24,128]{2,1,0:T(8,128)(2,1)}), bf16[48,384,128]{2,1,0:T(8,128)(2,1)}) %all-gather.7.cloned.1.call-update) | async-done | bytes 4718608 | tf_op jit(solution)/shard_map/all_gather | solution.py:117
  272.5 22.1 %copy.79 = bf16[48,384,128]{0,1,2:T(8,128)(2,1)} copy(bf16[48,384,128]{2,1,0:T(8,128)(2,1)} %all-gather.7.cloned.1.call-done) | data formatting | bytes 9437184 | tf_op jit(solution)/shard_map/all_gather | solution.py:117
  294.6 11.4 %convolution_bitcast_fusion.1 = f32[384,24,128]{0,1,2:T(8,128)} fusion(bf16[48,24,128]{0,1,2:T(8,128)(2,1)} %copy.78, bf16[48,384,128]{0,1,2:T(8,128)(2,1)} %copy.79), kind=kOutput, calls=%fused_computation.1 | convolution fusion | flops 113246208 | bytes 9732096 | tf_op jit(solution)/shard_map/kih,kjh->ijh/dot_general | solution.py:174
  306.1 6.1 copy.80
  312.2 98.3 %reduce-scatter.7.cloned.1.call-done = f32[48,24,128]{2,1,0:T(8,128)} async-done(((f32[384,24,128]{2,1,0:T(8,128)}), f32[48,24,128]{2,1,0:T(8,128)}) %reduce-scatter.7.cloned.1.call-update) | async-done | bytes 589840 | tf_op jit(solution)/shard_map/reduce_scatter | solution.py:130
  410.4 1.9 reduce_sum.150
  413.1 1.5 multiply_reduce_fusion.2
  414.7 2.1 fusion.109
  416.9 1.4 multiply_convert_fusion.11
  418.4 55.9 %all-gather.9.cloned.1.call-done = bf16[384,24,128]{2,1,0:T(8,128)(2,1)} async-done(((bf16[48,24,128]{2,1,0:T(8,128)(2,1)}), bf16[384,24,128]{2,1,0:T(8,128)(2,1)}) %all-gather.9.cloned.1.call-update) | async-done | bytes 2359312 | tf_op jit(solution)/shard_map/all_gather | solution.py:113
  474.3 4.7 copy.90
  479.1 7.0 fusion.111
  486.1 9.6 %copy.91 = f32[128,48,384]{0,2,1:T(8,128)} copy(f32[128,48,384]{2,1,0:T(8,128)} %fusion.111) | data formatting | bytes 18874368 | tf_op jit(solution)/shard_map/ijh,kjh->ikh/dot_general | solution.py:192
  496.0 8.8 %fusion.112 = f32[128,24,48]{2,1,0:T(8,128)} fusion(bf16[384,24,128]{0,1,2:T(8,128)(2,1)} %copy.90, bf16[48,384,128]{0,1,2:T(8,128)(2,1)} %copy.79), kind=kOutput, calls=%fused_computation.184 | convolution fusion | flops 113246208 | bytes 7667712 | tf_op jit(solution)/shard_map/kih,ijh->kjh/dot_general | solution.py:187
  504.8 2.7 copy.94
  507.5 96.2 %reduce-scatter.9.cloned.1.call-done = f32[24,48,128]{2,0,1:T(8,128)} async-done(((f32[384,48,128]{2,0,1:T(8,128)}), f32[24,48,128]{2,0,1:T(8,128)}) %reduce-scatter.9.cloned.1.call-update) | async-done | bytes 589840 | tf_op jit(solution)/shard_map/reduce_scatter | solution.py:121
  603.7 1.6 fusion.50
  605.3 1.8 fusion.51
  607.8 1.4 fusion.59
  610.3 3.4 fusion.107
  615.7 58.2 %all-gather.11.cloned.1.call-done = bf16[48,384,128]{2,0,1:T(8,128)(2,1)} async-done(((bf16[48,24,128]{2,0,1:T(8,128)(2,1)}), bf16[48,384,128]{2,0,1:T(8,128)(2,1)}) %all-gather.11.cloned.1.call-update) | async-done | bytes 4718608 | tf_op jit(solution)/shard_map/all_gather | solution.py:117
  673.9 17.8 %copy.97 = bf16[48,384,128]{0,1,2:T(8,128)(2,1)} copy(bf16[48,384,128]{2,0,1:T(8,128)(2,1)} %all-gather.11.cloned.1.call-done) | data formatting | bytes 9437184 | tf_op jit(solution)/shard_map/all_gather | solution.py:117
  691.7 11.2 %fusion.114 = f32[128,24,384]{2,1,0:T(8,128)} fusion(bf16[48,24,128]{0,1,2:T(8,128)(2,1)S(1)} %copy.74, bf16[48,384,128]{0,1,2:T(8,128)(2,1)} %copy.97), kind=kOutput, calls=%fused_computation.186 | convolution fusion | flops 113246208 | bytes 9732096 | tf_op jit(solution)/shard_map/ijh,ikh->jkh/dot_general | solution.py:218
  702.9 6.1 copy.101
  709.0 8.1 fusion.113
  717.0 2.0 copy.98
  719.1 2.1 fusion.54
  721.1 1.7 fusion.55
  722.9 84.5 %reduce-scatter.11.cloned.1.call-done = f32[48,24,128]{2,1,0:T(8,128)} async-done(((f32[384,24,128]{2,1,0:T(8,128)}), f32[48,24,128]{2,1,0:T(8,128)}) %reduce-scatter.11.cloned.1.call-update) | async-done | bytes 589840 | tf_op jit(solution)/shard_map/reduce_scatter | solution.py:130
  807.4 2.1 fusion.56
  809.6 2.2 fusion.57
  811.8 1.6 fusion.58
  813.5 2.1 fusion.106
  815.6 4.1 fusion.21
  (133 shorter events, 11.9 us)
Async XLA Ops:
  7.2 67.4 %all-gather.5.cloned.1.call-start = ((), (), s32[]{:S(2)}) async-start(), calls=%async_computation.4 | async-start | bytes 2654208 | tf_op jit(solution)/shard_map/all_gather | solution.py:113
  9.2 2.6 copy-start.25
  10.6 1.2 copy-start.30
  11.8 598.3 %copy-start.13 = (f32[48,24]{1,0:T(8,128)}, f32[48,24]{1,0:T(8,128)S(1)}, u32[]{:S(2)}) copy-start(f32[48,24]{1,0:T(8,128)S(1)} %fusion.101) | copy-start | bytes 13828
  13.6 1.7 copy-start
  16.4 184.8 %reduce-scatter.5.cloned.1.call-start = ((), (), s32[]{:S(2)}) async-start(), calls=%async_computation.5 | async-start | bytes 10027008 | tf_op jit(solution)/shard_map/reduce_scatter | solution.py:121
  93.2 110.9 %copy-start.8 = (bf16[48,24,128]{2,1,0:T(8,128)(2,1)S(1)}, bf16[48,24,128]{2,1,0:T(8,128)(2,1)}, u32[]{:S(2)}) copy-start(bf16[48,24,128]{2,1,0:T(8,128)(2,1)} %param.7) | copy-start | bytes 884740
  93.2 179.3 %all-gather.7.cloned.1.call-start = ((), (), s32[]{:S(2)}) async-start(), calls=%async_computation.6 | async-start | bytes 5013504 | tf_op jit(solution)/shard_map/all_gather | solution.py:117
  204.0 3.5 copy-start.27
  204.1 2.7 copy-start.38
  206.8 403.3 %copy-start.19 = (f32[48,24]{1,0:T(8,128)}, f32[48,24]{1,0:T(8,128)S(1)}, u32[]{:S(2)}) copy-start(f32[48,24]{1,0:T(8,128)S(1)} %broadcast_multiply_fusion.9) | copy-start | bytes 13828
  207.2 402.9 %copy-start.23 = (f32[48,24]{1,0:T(8,128)}, f32[48,24]{1,0:T(8,128)S(1)}, u32[]{:S(2)}) copy-start(f32[48,24]{1,0:T(8,128)S(1)} %add_rsqrt_fusion.1) | copy-start | bytes 13828
  208.3 1.6 copy-start.2
  211.0 199.4 %reduce-scatter.7.cloned.1.call-start = ((), (), s32[]{:S(2)}) async-start(), calls=%async_computation.7 | async-start | bytes 5308416 | tf_op jit(solution)/shard_map/reduce_scatter | solution.py:130
  312.1 102.6 %copy-start.17 = (bf16[48,24,128]{2,1,0:T(8,128)(2,1)S(1)}, bf16[48,24,128]{2,1,0:T(8,128)(2,1)}, u32[]{:S(2)}) copy-start(bf16[48,24,128]{2,1,0:T(8,128)(2,1)} %param.13) | copy-start | bytes 884740
  312.1 162.2 %all-gather.9.cloned.1.call-start = ((), (), s32[]{:S(2)}) async-start(), calls=%async_computation.8 | async-start | bytes 2654208 | tf_op jit(solution)/shard_map/all_gather | solution.py:113
  413.1 3.7 copy-start.36
  413.1 3.8 copy-start.5
  414.7 2.2 copy-start.40
  418.3 185.3 %reduce-scatter.9.cloned.1.call-start = ((), (), s32[]{:S(2)}) async-start(), calls=%async_computation.9 | async-start | bytes 10027008 | tf_op jit(solution)/shard_map/reduce_scatter | solution.py:121
  495.7 178.1 %all-gather.11.cloned.1.call-start = ((), (), s32[]{:S(2)}) async-start(), calls=%async_computation.10 | async-start | bytes 5013504 | tf_op jit(solution)/shard_map/all_gather | solution.py:117
  603.7 3.5 copy-start.3
  603.7 3.5 copy-start.7
  605.3 2.5 copy-start.6
  605.3 2.5 copy-start.37
  605.3 2.5 copy-start.41
  605.3 2.5 copy-start.43
  607.8 1.5 copy-start.11
  607.8 1.5 copy-start.28
  610.0 3.7 copy-start.15
  610.1 3.7 copy-start.32
  610.1 3.7 copy-start.34
  615.4 192.1 %reduce-scatter.11.cloned.1.call-start = ((), (), s32[]{:S(2)}) async-start(), calls=%async_computation.11 | async-start | bytes 5308416 | tf_op jit(solution)/shard_map/reduce_scatter | solution.py:130
  717.0 4.1 copy-start.1
  722.9 88.9 %copy-start.12 = (bf16[48,24,128]{2,1,0:T(8,128)(2,1)S(1)}, bf16[48,24,128]{2,1,0:T(8,128)(2,1)}, u32[]{:S(2)}) copy-start(bf16[48,24,128]{2,1,0:T(8,128)(2,1)} %copy-done.10) | copy-start | bytes 884740
  722.9 88.9 %copy-start.14 = (f32[48,24]{1,0:T(8,128)S(1)}, f32[48,24]{1,0:T(8,128)}, u32[]{:S(2)}) copy-start(f32[48,24]{1,0:T(8,128)} %copy-done.13) | copy-start | bytes 13828
  722.9 88.9 %copy-start.20 = (f32[48,24]{1,0:T(8,128)S(1)}, f32[48,24]{1,0:T(8,128)}, u32[]{:S(2)}) copy-start(f32[48,24]{1,0:T(8,128)} %copy-done.19) | copy-start | bytes 13828
  722.9 88.9 %copy-start.24 = (f32[48,24]{1,0:T(8,128)S(1)}, f32[48,24]{1,0:T(8,128)}, u32[]{:S(2)}) copy-start(f32[48,24]{1,0:T(8,128)} %copy-done.23) | copy-start | bytes 13828
  722.9 88.9 %copy-start.33 = (f32[48,24]{1,0:T(8,128)S(1)}, f32[48,24]{1,0:T(8,128)}, u32[]{:S(2)}) copy-start(f32[48,24]{1,0:T(8,128)} %copy-done.32) | copy-start | bytes 13828
  722.9 88.9 %copy-start.35 = (f32[48,24]{1,0:T(8,128)S(1)}, f32[48,24]{1,0:T(8,128)}, u32[]{:S(2)}) copy-start(f32[48,24]{1,0:T(8,128)} %copy-done.34) | copy-start | bytes 13828
  807.4 4.4 copy-start.16
  807.4 4.4 copy-start.18
  807.4 4.4 copy-start.21
  809.6 3.9 copy-start.9
  809.6 3.9 copy-start.26
  809.6 3.9 copy-start.29
  809.6 3.9 copy-start.31
  811.8 3.8 copy-start.22
  (4 other events, 3.5 us)
Sparse Core Ops, SparseCore 0:
  16.5 58.0 all-gather.4
  93.4 107.8 reduce-scatter.4
  211.1 61.3 all-gather.6
  312.3 98.1 reduce-scatter.6
  418.5 55.8 all-gather.8
  495.8 107.7 reduce-scatter.8
  615.5 58.3 all-gather.10
  709.1 98.3 reduce-scatter.10
where the time goes:
time: 828 us; the launch traced here: 827 us
  waiting for transfers between devices  618 us (75%)
  local copies, waits for them, and re-layouts  92.5 us (11%)
  matrix products  67.9 us (8%)
  other arithmetic  32.2 us (4%)
  between operations  14.8 us (2%)
    reduce_scatter x2, waiting for transfers between devices, sum_cols(): lax.psum_scatter(term_fn(jnp.int32(0), row_total * lax.axis_size('col')),...  204 us
    reduce_scatter x2, waiting for transfers between devices, sum_rows(): lax.psum_scatter(term_fn(jnp.int32(0), row_total * lax.axis_size('row')),...  183 us
    all_gather x2, waiting for transfers between devices, gather_cols(): return lax.all_gather(block, 'col', axis=1, tiled=True)  118 us
    all_gather x2, waiting for transfers between devices, gather_rows(): return lax.all_gather(block, 'row', axis=0, tiled=True)  114 us
    all_gather x2, local copies, waits for them, and re-layouts, gather_cols(): return lax.all_gather(block, 'col', axis=1, tiled=True)  39.9 us
  transfers between devices with their start and end apart: 8, of which 8 were waited for; matrix products, arithmetic and copies ran while one was open for 3% of the time, Pallas kernels for 0%

commit v1 on v0

v1 whole, which is shorter than its diff:
```python
import functools

import jax
import jax.numpy as jnp
from jax import lax
from jax.experimental import pallas as pl
from jax.experimental.pallas import tpu as pltpu
from jax.sharding import PartitionSpec as P

RES = 384
TILES = 3
TILE = RES // TILES
CH = 128
ROWS = 8
COLS = 16
A = RES // ROWS
B = RES // COLS
PAIRS = A * B
NB = 8
CHUNK = NB * A
F32 = jnp.float32
BF16 = jnp.bfloat16
EPS = 1e-05
AXES = ("row", "col")
VM = pl.BlockSpec(memory_space=pltpu.VMEM)
SM = pl.BlockSpec(memory_space=pltpu.SMEM)


def normalize(values):
    center = values - jnp.mean(values, axis=-1, keepdims=True)
    inv = lax.rsqrt(jnp.mean(center * center, axis=-1, keepdims=True) + EPS)
    return center * inv, inv


def norm_back(standard, inv, gain, upstream):
    scaled = upstream * gain
    return inv * (
        scaled
        - jnp.mean(scaled, axis=-1, keepdims=True)
        - standard * jnp.mean(scaled * standard, axis=-1, keepdims=True)
    )


def mm(x, w):
    return lax.dot_general(x, w, (((1,), (0,)), ((), ())), preferred_element_type=F32)


def mm_nt(x, w):
    return lax.dot_general(x, w, (((1,), (1,)), ((), ())), preferred_element_type=F32)


def mm_tn(x, w):
    return lax.dot_general(x, w, (((0,), (0,)), ((), ())), preferred_element_type=F32)


def gate_chunk(mask_ref, b0):
    row_first = lax.axis_index("row") * A
    col_first = lax.axis_index("col") * B
    t0 = row_first // TILE
    t1 = jnp.minimum(t0 + 1, TILES - 1)
    low = lax.broadcasted_iota(jnp.int32, (A, CH), 0) < (t0 + 1) * TILE - row_first
    parts = []
    for k in range(NB):
        jt = (col_first + b0 + k) // TILE
        m0 = mask_ref[t0, jt].astype(F32)
        m1 = mask_ref[t1, jt].astype(F32)
        parts.append(jnp.where(low, jnp.full((A, CH), m0, F32), jnp.full((A, CH), m1, F32)))
    return jnp.concatenate(parts, axis=0)


def rows_of(chunk):
    return pl.ds(pl.multiple_of(chunk * CHUNK, CHUNK), CHUNK)


def load_turned(ref, b0):
    return jnp.concatenate([ref[pl.ds(b0 + k, A, stride=B), :] for k in range(NB)], axis=0)


def store_turned(ref, b0, value):
    for k in range(NB):
        ref[pl.ds(b0 + k, A, stride=B), :] = value[k * A:(k + 1) * A]


def pack_two(ref, b0, left, right):
    fill = jnp.zeros((CH - 2 * A, CH), F32)
    for k in range(NB):
        block = jnp.concatenate(
            [left[k * A:(k + 1) * A], right[k * A:(k + 1) * A], fill], axis=0
        )
        ref[pl.ds(b0 + k, CH, stride=B), :] = jnp.transpose(block)


def pack_one(ref, src):
    for b in range(16):
        first = src[pl.ds(b * A, A), :]
        if b < 8:
            second = src[pl.ds((b + 16) * A, A), :]
        else:
            second = jnp.zeros((A, CH), F32)
        block = jnp.concatenate([first, second, jnp.zeros((CH - 2 * A, CH), F32)], axis=0)
        ref[pl.ds(b, CH, stride=16), :] = jnp.transpose(block)


def unpack_one(msg_ref, wide, dst):
    wide[...] = msg_ref[...].astype(F32)
    for b in range(16):
        block = jnp.transpose(wide[pl.ds(b, CH, stride=16), :])
        dst[pl.ds(b * A, A), :] = block[:A]
        if b < 8:
            dst[pl.ds((b + 16) * A, A), :] = block[A:2 * A]


def unpack_two(wide, b0):
    lefts, rights = [], []
    for k in range(NB):
        block = jnp.transpose(wide[pl.ds(b0 + k, CH, stride=B), :])
        lefts.append(block[:A])
        rights.append(block[A:2 * A])
    return jnp.concatenate(lefts, axis=0), jnp.concatenate(rights, axis=0)


def sides(gate, proj):
    left = gate * jax.nn.sigmoid(proj[:, CH:2 * CH]) * proj[:, :CH]
    right = gate * jax.nn.sigmoid(proj[:, 3 * CH:4 * CH]) * proj[:, 2 * CH:3 * CH]
    return left, right


def chunks(fn):
    def step(i, carry):
        fn(i, i * NB)
        return carry

    lax.fori_loop(0, B // NB, step, 0)


def k_first(mask_ref, pair_ref, win_ref, gin_ref, msg_ref, x_ref, normed_ref, wide, msgf):
    wide[...] = pair_ref[...].astype(F32)

    def chunk(i, b0):
        gate = gate_chunk(mask_ref, b0)
        x = load_turned(wide, b0)
        x_ref[rows_of(i), :] = x.astype(BF16)
        standard, _ = normalize(x)
        normed = (standard * gin_ref[0:1, :]).astype(BF16)
        normed_ref[rows_of(i), :] = normed
        proj = mm(normed, win_ref[0, :, :4 * CH])
        left, right = sides(gate, proj)
        pack_two(msgf, b0, left, right)

    chunks(chunk)
    msg_ref[...] = msgf[...].astype(BF16)


def k_second(
    mask_ref, in_ref, x_ref, normed_ref, win_ref, wout_ref, gin_ref, gout_ref,
    msg_ref, inner_ref, mid_ref, normed1_ref, wide, inner, msgf,
):
    unpack_one(in_ref, wide, inner)

    def chunk(i, b0):
        gate = gate_chunk(mask_ref, b0)
        rows = rows_of(i)
        value = inner[rows, :]
        inner_ref[rows, :] = value.astype(BF16)
        standard, _ = normalize(value)
        update = mm((standard * gout_ref[0:1, :]).astype(BF16), wout_ref[0])
        sig = jax.nn.sigmoid(mm(normed_ref[rows, :], win_ref[0, :, 4 * CH:]))
        middle = (x_ref[rows, :].astype(F32) + gate * sig * update).astype(BF16)
        mid_ref[rows, :] = middle
        standard, _ = normalize(middle.astype(F32))
        normed = (standard * gin_ref[1:2, :]).astype(BF16)
        normed1_ref[rows, :] = normed
        left, right = sides(gate, mm(normed, win_ref[1, :, :4 * CH]))
        pack_two(msgf, b0, left, right)

    chunks(chunk)
    msg_ref[...] = msgf[...].astype(BF16)


def top_back(upstream, gate, normed, inner_value, u, win_ref, wout_ref, gout_ref):
    sig = jax.nn.sigmoid(mm(normed, win_ref[u, :, 4 * CH:]))
    gain = gout_ref[u:u + 1, :]
    standard, inv = normalize(inner_value)
    update = mm((standard * gain).astype(BF16), wout_ref[u])
    gated = upstream * gate
    d_update = (gated * sig).astype(BF16)
    d_gate = gated * update * sig * (1.0 - sig)
    d_inner = norm_back(standard, inv, gain, mm_nt(d_update, wout_ref[u]))
    return sig * update, d_gate, d_inner


def bottom_back(d_left, d_right, d_gate, gate, normed, state, u, win_ref, gin_ref):
    proj = mm(normed, win_ref[u, :, :4 * CH])
    left_sig = jax.nn.sigmoid(proj[:, CH:2 * CH])
    right_sig = jax.nn.sigmoid(proj[:, 3 * CH:4 * CH])
    d_left = d_left * gate * left_sig
    d_right = d_right * gate * right_sig
    d_proj = jnp.concatenate(
        [
            d_left.astype(BF16),
            (d_left * proj[:, :CH] * (1.0 - left_sig)).astype(BF16),
            d_right.astype(BF16),
            (d_right * proj[:, 2 * CH:3 * CH] * (1.0 - right_sig)).astype(BF16),
            d_gate,
        ],
        axis=1,
    )
    d_normed = mm_nt(d_proj, win_ref[u])
    standard, inv = normalize(state.astype(F32))
    return norm_back(standard, inv, gin_ref[u:u + 1, :], d_normed)


def k_third(
    mask_ref, in_ref, mid_ref, normed1_ref, cot_ref, win_ref, wout_ref, gout_ref,
    msg_ref, out_ref, cot_out_ref, dgate_ref, wide, inner, cotf, outf, msgf,
):
    unpack_one(in_ref, wide, inner)
    cotf[...] = cot_ref[...].astype(F32)

    def chunk(i, b0):
        gate = gate_chunk(mask_ref, b0)
        rows = rows_of(i)
        grad = load_turned(cotf, b0)
        cot_out_ref[rows, :] = grad.astype(BF16)
        gated_update, d_gate, d_inner = top_back(
            grad, gate, normed1_ref[rows, :], inner[rows, :], 1, win_ref, wout_ref, gout_ref
        )
        store_turned(outf, b0, mid_ref[rows, :].astype(F32) + gate * gated_update)
        dgate_ref[rows, :] = d_gate.astype(BF16)
        inner[rows, :] = d_inner

    chunks(chunk)
    out_ref[...] = outf[...].astype(BF16)
    pack_one(msgf, inner)
    msg_ref[...] = msgf[...].astype(BF16)


def k_fourth(
    mask_ref, in_ref, mid_ref, normed1_ref, cot_ref, dgate1_ref, inner0_ref, normed0_ref,
    win_ref, wout_ref, gin_ref, gout_ref,
    msg_ref, grad_ref, dgate_ref, wide, inner, msgf,
):
    wide[...] = in_ref[...].astype(F32)

    def chunk(i, b0):
        gate = gate_chunk(mask_ref, b0)
        rows = rows_of(i)
        d_left, d_right = unpack_two(wide, b0)
        grad = cot_ref[rows, :].astype(F32) + bottom_back(
            d_left, d_right, dgate1_ref[rows, :], gate, normed1_ref[rows, :], mid_ref[rows, :],
            1, win_ref, gin_ref,
        )
        grad_ref[rows, :] = grad
        _, d_gate, d_inner = top_back(
            grad, gate, normed0_ref[rows, :], inner0_ref[rows, :].astype(F32), 0,
            win_ref, wout_ref, gout_ref,
        )
        dgate_ref[rows, :] = d_gate.astype(BF16)
        inner[rows, :] = d_inner

    chunks(chunk)
    pack_one(msgf, inner)
    msg_ref[...] = msgf[...].astype(BF16)


def k_fifth(
    mask_ref, in_ref, x_ref, normed0_ref, grad_ref, dgate0_ref, win_ref, gin_ref,
    out_ref, wide,
):
    wide[...] = in_ref[...].astype(F32)

    def chunk(i, b0):
        gate = gate_chunk(mask_ref, b0)
        rows = rows_of(i)
        d_left, d_right = unpack_two(wide, b0)
        grad = grad_ref[rows, :] + bottom_back(
            d_left, d_right, dgate0_ref[rows, :], gate, normed0_ref[rows, :], x_ref[rows, :],
            0, win_ref, gin_ref,
        )
        store_turned(out_ref, b0, grad)

    chunks(chunk)


def lanes(n):
    return lax.broadcasted_iota(jnp.int32, (n, 128), 1)


def turn(value, shift):
    shift = shift % 128
    return value if shift == 0 else pltpu.roll(value, shift, axis=1)


def spread(pieces):
    lane = lanes(pieces[0].shape[0])
    tiles = []
    for t in range(3):
        inside = [r for r in range(ROWS) if r * A < (t + 1) * 128 and (r + 1) * A > t * 128]
        tile = pieces[inside[-1]]
        for r in reversed(inside[:-1]):
            tile = jnp.where(lane < (r + 1) * A - t * 128, pieces[r], tile)
        tiles.append(tile)
    return tiles


def cut(tiles, r, place):
    t, off = divmod(r * A, 128)
    if off + A <= 128:
        return turn(tiles[t], place - off)
    lane = lanes(tiles[t].shape[0])
    both = jnp.where(lane >= off, tiles[t], tiles[t + 1])
    return turn(both, place - off)


STEP = 48


def join_two(x_ref, lt, rt):
    for s in range(RES // STEP):
        blocks = [x_ref[r * RES + s * STEP:r * RES + (s + 1) * STEP, :].astype(F32) for r in range(ROWS)]
        for dst, start in ((lt, 0), (rt, A)):
            tiles = spread([turn(v, r * A - start) for r, v in enumerate(blocks)])
            for t in range(3):
                dst[s * STEP:(s + 1) * STEP, t * 128:(t + 1) * 128] = tiles[t].astype(BF16)


def join_one(x_ref, dst):
    for c in range(0, COLS, 2):
        rows = [[], [], []]
        for cc in (c, c + 1):
            blocks = [x_ref[(r * COLS + cc) * 16:(r * COLS + cc) * 16 + 16, :].astype(F32) for r in range(ROWS)]
            top = spread([turn(v, r * A) for r, v in enumerate(blocks)])
            end = spread([turn(v[:8], r * A - A) for r, v in enumerate(blocks)])
            for t in range(3):
                rows[t] += [top[t], end[t]]
        for t in range(3):
            dst[c * B:(c + 2) * B, t * 128:(t + 1) * 128] = jnp.concatenate(rows[t], axis=0).astype(BF16)


def split_two(lt, rt, o_ref):
    for s in range(RES // STEP):
        rows = slice(s * STEP, (s + 1) * STEP)
        left = [lt[rows, t * 128:(t + 1) * 128] for t in range(3)]
        right = [rt[rows, t * 128:(t + 1) * 128] for t in range(3)]
        lane = lanes(STEP)
        for r in range(ROWS):
            block = jnp.where(lane < A, cut(left, r, 0), cut(right, r, A))
            o_ref[r * RES + s * STEP:r * RES + (s + 1) * STEP, :] = block.astype(BF16)


def split_one(value, o_ref):
    for c in range(COLS):
        tiles = [value[c * B:(c + 1) * B, t * 128:(t + 1) * 128] for t in range(3)]
        lane = lanes(8)
        for r in range(ROWS):
            top = cut([v[:16] for v in tiles], r, 0)
            end = cut([v[16:] for v in tiles], r, A)
            block = jnp.concatenate([jnp.where(lane < A, top[:8], end), top[8:]], axis=0)
            o_ref[(r * COLS + c) * 16:(r * COLS + c) * 16 + 16, :] = block.astype(BF16)


def m_forward(u, x_ref, o_ref, lt, rt, prod):
    join_two(x_ref, lt, rt)
    if u == 0:
        prod[...] = mm_tn(rt[...], lt[...])
    else:
        prod[...] = mm_nt(rt[...], lt[...])
    split_one(prod, o_ref)


def m_backward(u, x_ref, lt, rt, o_ref, dt, prod_l, prod_r):
    join_one(x_ref, dt)
    if u == 0:
        prod_l[...] = mm(rt[...], dt[...])
        prod_r[...] = mm_nt(lt[...], dt[...])
    else:
        prod_l[...] = mm_tn(dt[...], rt[...])
        prod_r[...] = mm(dt[...], lt[...])
    split_two(prod_l, prod_r, o_ref)


def shape(*dims, dtype=BF16):
    return jax.ShapeDtypeStruct(dims, dtype)


def call(fn, outs, scratch, name, smem=True):
    def run(*args):
        specs = ([SM] if smem else []) + [VM] * (len(args) - (1 if smem else 0))
        return pl.pallas_call(
            fn,
            out_shape=outs,
            in_specs=specs,
            out_specs=[VM] * len(outs),
            scratch_shapes=scratch,
            compiler_params=pltpu.CompilerParams(vmem_limit_bytes=24 * 1024 * 1024),
            name=name,
        )(*args)

    return run


def exchange(message, rows):
    message = message.reshape(ROWS * COLS, rows, 128)
    return lax.all_to_all(message, AXES, 0, 0, tiled=True).reshape(ROWS * COLS * rows, 128)


TWO = (CH * B, 128)
ONE = (CH * 16, 128)
PAIR = (PAIRS, CH)
FULL = (RES, RES)


def wide(dims):
    return pltpu.VMEM(dims, F32)


def body(pair_state, tile_mask, weight_in, weight_out, gain_in, gain_out, cotangent):
    msg, x, normed0 = call(
        k_first, (shape(*TWO), shape(*PAIR), shape(*PAIR)), [wide(PAIR), wide(TWO)], "first"
    )(tile_mask, pair_state.reshape(PAIRS, CH), weight_in, gain_in)
    msg = exchange(msg, B)
    msg, lt0, rt0 = call(
        functools.partial(m_forward, 0), (shape(*ONE), shape(*FULL), shape(*FULL)),
        [wide(FULL)], "product0", smem=False,
    )(msg)
    msg = exchange(msg, 16)
    msg, inner0, middle, normed1 = call(
        k_second, (shape(*TWO), shape(*PAIR), shape(*PAIR), shape(*PAIR)),
        [wide(ONE), wide(PAIR), wide(TWO)], "second",
    )(tile_mask, msg, x, normed0, weight_in, weight_out, gain_in, gain_out)
    msg = exchange(msg, B)
    msg, lt1, rt1 = call(
        functools.partial(m_forward, 1), (shape(*ONE), shape(*FULL), shape(*FULL)),
        [wide(FULL)], "product1", smem=False,
    )(msg)
    msg = exchange(msg, 16)
    msg, updated, cot, dgate1 = call(
        k_third, (shape(*ONE), shape(*PAIR), shape(*PAIR), shape(*PAIR)),
        [wide(ONE), wide(PAIR), wide(PAIR), wide(PAIR), wide(ONE)], "third",
    )(tile_mask, msg, middle, normed1, cotangent.reshape(PAIRS, CH), weight_in, weight_out, gain_out)
    msg = exchange(msg, 16)
    (msg,) = call(
        functools.partial(m_backward, 1), (shape(*TWO),),
        [pltpu.VMEM(FULL, BF16), wide(FULL), wide(FULL)], "back1", smem=False,
    )(msg, lt1, rt1)
    msg = exchange(msg, B)
    msg, grad, dgate0 = call(
        k_fourth, (shape(*ONE), shape(*PAIR, dtype=F32), shape(*PAIR)),
        [wide(TWO), wide(PAIR), wide(ONE)], "fourth",
    )(tile_mask, msg, middle, normed1, cot, dgate1, inner0, normed0, weight_in, weight_out, gain_in, gain_out)
    msg = exchange(msg, 16)
    (msg,) = call(
        functools.partial(m_backward, 0), (shape(*TWO),),
        [pltpu.VMEM(FULL, BF16), wide(FULL), wide(FULL)], "back0", smem=False,
    )(msg, lt0, rt0)
    msg = exchange(msg, B)
    (pair_grad,) = call(
        k_fifth, (shape(*PAIR, dtype=F32),), [wide(TWO)], "fifth"
    )(tile_mask, msg, x, normed0, grad, dgate0, weight_in, gain_in)
    return updated.reshape(A, B, CH), pair_grad.reshape(A, B, CH)


def solution(mesh):
    return jax.shard_map(
        body,
        mesh=mesh,
        in_specs=(P("row", "col", None), P(), P(), P(), P(), P(), P("row", "col", None)),
        out_specs=(P("row", "col", None), P("row", "col", None)),
        check_vma=False,
    )
```

time: 828 us -> 185 us (0.22)
  waiting for transfers between devices: 618 us -> 0 us
  blocking collectives: 0 us -> 159 us
  local copies, waits for them, and re-layouts: 92.5 us -> 3.99 us
  matrix products: 67.9 us -> 0 us
  other arithmetic: 32.2 us -> 0 us
  Pallas kernels: 0 us -> 20.8 us
  between operations: 14.8 us -> 0.73 us
    reduce_scatter x4 -> x0, waiting for transfers between devices: 386 us -> none  [the longest x2 204 us: sum_cols(): lax.psum_scatter(term_fn(jnp.int32(0), row_total * lax.axis_size('col')),...]
    all_gather x4 -> x0, waiting for transfers between devices: 232 us -> none  [the longest x2 118 us: gather_cols(): return lax.all_gather(block, 'col', axis=1, tiled=True)]
    all_to_all x0 -> x8, blocking collectives: none -> 159 us  [exchange(): lax.all_to_all(message, AXES, 0, 0, tiled=True)]
    dot_general x16 -> x0, matrix products: 67.9 us -> none  [the longest x1 11.4 us: second_terms(): jnp.einsum('kih,kjh->ijh', left_rows_second, right_second, preferred_elem...]
    all_gather x4 -> x0, local copies, waits for them, and re-layouts: 48.4 us -> none  [the longest x2 39.9 us: gather_cols(): return lax.all_gather(block, 'col', axis=1, tiled=True)]
    pallas_call x0 -> x9, Pallas kernels: none -> 20.8 us  [run(): pl.pallas_call(fn, out_shape=outs, in_specs=specs, out_specs=[VM] * len(o...]
    dot_general x4 -> x0, local copies, waits for them, and re-layouts: 20.4 us -> none  [the longest x1 9.62 us: second_back_terms(): jnp.einsum('ijh,kjh->ikh', grad_cols, right_second, preferred_element_typ...]
    transpose x2 -> x0, local copies, waits for them, and re-layouts: 15.8 us -> none  [the longest x1 9.79 us: front_terms(): jnp.einsum('jkh,ikh->jih', right_every, left_front, preferred_element_typ...]
  transfers between devices with their start and end apart: 8 -> 0, of which waited for: 8 -> 0; matrix products, arithmetic and copies ran while one was open for 3% -> 0% of each run, Pallas kernels for 0% -> 0%
where the time goes in v1:
time: 185 us; the launch traced here: 184 us
  blocking collectives  159 us (86%)
  Pallas kernels  20.8 us (11%)
  local copies, waits for them, and re-layouts  3.99 us (2%)
    all_to_all x8, blocking collectives, exchange(): lax.all_to_all(message, AXES, 0, 0, tiled=True)  159 us
    pallas_call x9, Pallas kernels, run(): pl.pallas_call(fn, out_shape=outs, in_specs=specs, out_specs=[VM] * len(o...  20.8 us
    unnamed x18, local copies, waits for them, and re-layouts  3.99 us

profile of v1, /device:TPU:1, one launch (start us, length us, event | category | flops | bytes accessed | tf_op | source)
XLA Modules:
  0.0 184.4 jit_solution(10194575491653977266)
XLA Ops:
  0.6 0.0 copy-start.7
  0.6 0.7 copy-done.7
  1.3 0.0 copy-start
  1.3 1.0 copy-done
  2.3 0.0 copy-start.3
  2.3 1.0 copy-done.3
  3.2 0.0 copy-start.5
  3.2 0.7 copy-done.5
  3.9 2.5 %first.1 = (bf16[3072,128]{1,0:T(8,128)(2,1)S(1)}, bf16[1152,128]{1,0:T(8,128)(2,1)S(1)}, bf16[1152,128]{1,0:T(8,128)(2,1)S(1)}) custom-call(s32[3,3]{1,0:T(4,128)S(1)} %copy-done.5, bf16[1152,128]{1,0:T(8,128)(2,1)S(1)} %bitcast.36, bf16[2,128,640]{2,1,0:T(8,128)(2,1)S(1)} %copy-done, f32[2,128]{1,0:T(2,128)S(1)} %copy-done.7), custom_call_target="tpu_custom_call" | custom-call | tf_op jit(solution)/shard_map/first/pallas_call | solution.py:389
  6.4 27.5 %all_to_all.40 = bf16[128,24,128]{2,1,0:T(8,128)(2,1)S(1)} all-to-all(bf16[128,24,128]{2,1,0:T(8,128)(2,1)S(1)} %bitcast.31), channel_id=1, replica_groups=mesh['row'=8,'col'=16] {'row','col'}, dimensions={0} | all-to-all | bytes 1572864 | tf_op jit(solution)/shard_map/all_to_all | solution.py:404
  33.9 1.0 product0.1
  34.9 0.0 copy-start.1
  35.0 0.0 copy-start.2
  35.0 17.8 %all_to_all.41 = bf16[128,16,128]{2,1,0:T(8,128)(2,1)S(1)} all-to-all(bf16[128,16,128]{2,1,0:T(8,128)(2,1)S(1)} %bitcast.34), channel_id=1, replica_groups=mesh['row'=8,'col'=16] {'row','col'}, dimensions={0} | all-to-all | bytes 1048576 | tf_op jit(solution)/shard_map/all_to_all | solution.py:404
  52.7 0.0 copy-start.6
  52.7 0.0 copy-start.8
  52.7 0.0 copy-done.1
  52.7 0.0 copy-done.2
  52.7 0.7 copy-done.6
  53.4 0.0 copy-done.8
  53.4 3.8 %second.1 = (bf16[3072,128]{1,0:T(8,128)(2,1)S(1)}, bf16[1152,128]{1,0:T(8,128)(2,1)S(1)}, bf16[1152,128]{1,0:T(8,128)(2,1)S(1)}, bf16[1152,128]{1,0:T(8,128)(2,1)S(1)}) custom-call(s32[3,3]{1,0:T(4,128)S(1)} %copy-done.6, bf16[2048,128]{1,0:T(8,128)(2,1)S(1)} %bitcast.26, bf16[1152,128]{1,0:T(8,128)(2,1)S(1)} %get-tuple-element.24.x_ref, ...), custom_call_target="tpu_custom_call" | custom-call | tf_op jit(solution)/shard_map/second/pallas_call | solution.py:389
  57.2 20.2 %all_to_all.42 = bf16[128,24,128]{2,1,0:T(8,128)(2,1)S(1)} all-to-all(bf16[128,24,128]{2,1,0:T(8,128)(2,1)S(1)} %bitcast.30), channel_id=1, replica_groups=mesh['row'=8,'col'=16] {'row','col'}, dimensions={0} | all-to-all | bytes 1572864 | tf_op jit(solution)/shard_map/all_to_all | solution.py:404
  77.4 1.0 product1.1
  78.4 0.0 copy-start.4
  78.4 17.8 %all_to_all.43 = bf16[128,16,128]{2,1,0:T(8,128)(2,1)S(1)} all-to-all(bf16[128,16,128]{2,1,0:T(8,128)(2,1)S(1)} %bitcast.35), channel_id=1, replica_groups=mesh['row'=8,'col'=16] {'row','col'}, dimensions={0} | all-to-all | bytes 1048576 | tf_op jit(solution)/shard_map/all_to_all | solution.py:404
  96.2 0.0 copy-done.4
  96.2 3.6 %third.1 = (bf16[2048,128]{1,0:T(8,128)(2,1)S(1)}, bf16[1152,128]{1,0:T(8,128)(2,1)}, bf16[1152,128]{1,0:T(8,128)(2,1)S(1)}, bf16[1152,128]{1,0:T(8,128)(2,1)S(1)}) custom-call(s32[3,3]{1,0:T(4,128)S(1)} %copy-done.6, bf16[2048,128]{1,0:T(8,128)(2,1)S(1)} %bitcast.27, bf16[1152,128]{1,0:T(8,128)(2,1)S(1)} %get-tuple-element.28.mid_ref, ...), custom_call_target="tpu_custom_call" | custom-call | tf_op jit(solution)/shard_map/third/pallas_call | solution.py:389
  99.8 17.5 %all_to_all.44 = bf16[128,16,128]{2,1,0:T(8,128)(2,1)S(1)} all-to-all(bf16[128,16,128]{2,1,0:T(8,128)(2,1)S(1)} %bitcast.33), channel_id=1, replica_groups=mesh['row'=8,'col'=16] {'row','col'}, dimensions={0} | all-to-all | bytes 1048576 | tf_op jit(solution)/shard_map/all_to_all | solution.py:404
  117.3 1.0 back1.1
  118.3 20.2 %all_to_all.45 = bf16[128,24,128]{2,1,0:T(8,128)(2,1)S(1)} all-to-all(bf16[128,24,128]{2,1,0:T(8,128)(2,1)S(1)} %bitcast.24), channel_id=1, replica_groups=mesh['row'=8,'col'=16] {'row','col'}, dimensions={0} | all-to-all | bytes 1572864 | tf_op jit(solution)/shard_map/all_to_all | solution.py:404
  138.5 3.8 %fourth.1 = (bf16[2048,128]{1,0:T(8,128)(2,1)S(1)}, f32[1152,128]{1,0:T(8,128)S(1)}, bf16[1152,128]{1,0:T(8,128)(2,1)S(1)}) custom-call(s32[3,3]{1,0:T(4,128)S(1)} %copy-done.6, bf16[3072,128]{1,0:T(8,128)(2,1)S(1)} %bitcast.22, bf16[1152,128]{1,0:T(8,128)(2,1)S(1)} %get-tuple-element.28.mid_ref, bf16[1152,128]{1,0:T(8,128)(2,1)S(1)} %get-tuple-element.29.normed1_ref, ...), custom_call_target="tpu_custom_call" | custom-call | tf_op jit(solution)/shard_map/fourth/pallas_call | solution.py:389
  142.3 17.6 %all_to_all.46 = bf16[128,16,128]{2,1,0:T(8,128)(2,1)S(1)} all-to-all(bf16[128,16,128]{2,1,0:T(8,128)(2,1)S(1)} %bitcast.32), channel_id=1, replica_groups=mesh['row'=8,'col'=16] {'row','col'}, dimensions={0} | all-to-all | bytes 1048576 | tf_op jit(solution)/shard_map/all_to_all | solution.py:404
  160.0 0.9 back0.1
  160.9 20.2 %all_to_all.47 = bf16[128,24,128]{2,1,0:T(8,128)(2,1)S(1)} all-to-all(bf16[128,24,128]{2,1,0:T(8,128)(2,1)S(1)} %bitcast.25), channel_id=1, replica_groups=mesh['row'=8,'col'=16] {'row','col'}, dimensions={0} | all-to-all | bytes 1572864 | tf_op jit(solution)/shard_map/all_to_all | solution.py:404
  181.1 3.3 %fifth.1 = f32[1152,128]{1,0:T(8,128)} custom-call(s32[3,3]{1,0:T(4,128)S(1)} %copy-done.6, bf16[3072,128]{1,0:T(8,128)(2,1)S(1)} %bitcast.23, bf16[1152,128]{1,0:T(8,128)(2,1)S(1)} %get-tuple-element.24.x_ref, bf16[1152,128]{1,0:T(8,128)(2,1)S(1)} %get-tuple-element.25.normed_ref.normed0_ref, f32[1152,128]{1,0:T(8,128)S(1)} %get-tuple-element.40.grad_ref, ...), custom_call_target="tpu_custom_call" | custom-call | tf_op jit(solution)/shard_map/fifth/pallas_call | solution.py:389
Async XLA Ops:
  0.6 0.7 copy-start.7
  1.3 1.0 copy-start
  2.3 1.0 copy-start.3
  3.2 0.7 copy-start.5
  34.9 17.8 %copy-start.1 = (bf16[2,128,640]{2,1,0:T(8,128)(2,1)S(1)}, bf16[2,128,640]{2,1,0:T(8,128)(2,1)}, u32[]{:S(2)}) copy-start(bf16[2,128,640]{2,1,0:T(8,128)(2,1)} %win_ref.9) | copy-start | bytes 983044
  35.0 17.8 %copy-start.2 = (bf16[2,128,128]{2,1,0:T(8,128)(2,1)S(1)}, bf16[2,128,128]{2,1,0:T(8,128)(2,1)}, u32[]{:S(2)}) copy-start(bf16[2,128,128]{2,1,0:T(8,128)(2,1)} %wout_ref.5) | copy-start | bytes 196612
  52.7 0.7 copy-start.6
  52.7 0.7 copy-start.8
  78.4 17.8 %copy-start.4 = (bf16[48,24,128]{2,1,0:T(8,128)(2,1)S(1)}, bf16[48,24,128]{2,1,0:T(8,128)(2,1)}, u32[]{:S(2)}) copy-start(bf16[48,24,128]{2,1,0:T(8,128)(2,1)} %param.13) | copy-start | bytes 884740

commit v2 on v1

v2 whole, which is shorter than its diff:
```python
import functools

import jax
import jax.numpy as jnp
from jax import lax
from jax.experimental import pallas as pl
from jax.experimental.pallas import tpu as pltpu
from jax.sharding import PartitionSpec as P

RES = 384
TILES = 3
TILE = RES // TILES
CH = 128
ROWS = 8
COLS = 16
A = RES // ROWS
B = RES // COLS
PAIRS = A * B
NB = 8
CHUNK = NB * A
F32 = jnp.float32
BF16 = jnp.bfloat16
EPS = 1e-05
AXES = ("row", "col")
VM = pl.BlockSpec(memory_space=pltpu.VMEM)
SM = pl.BlockSpec(memory_space=pltpu.SMEM)
HB = pl.BlockSpec(memory_space=pltpu.HBM)
DMA = pltpu.SemaphoreType.DMA
TWO_ROWS = 18
ONE_ROWS = 10


def mm(x, w):
    return lax.dot_general(x, w, (((1,), (0,)), ((), ())), preferred_element_type=F32)


def mm_nt(x, w):
    return lax.dot_general(x, w, (((1,), (1,)), ((), ())), preferred_element_type=F32)


def mm_tn(x, w):
    return lax.dot_general(x, w, (((0,), (0,)), ((), ())), preferred_element_type=F32)


def gate_chunk(mask_ref, b0):
    row_first = lax.axis_index("row") * A
    col_first = lax.axis_index("col") * B
    t0 = row_first // TILE
    t1 = jnp.minimum(t0 + 1, TILES - 1)
    low = lax.broadcasted_iota(jnp.int32, (A, CH), 0) < (t0 + 1) * TILE - row_first
    parts = []
    for k in range(NB):
        jt = (col_first + b0 + k) // TILE
        m0 = mask_ref[t0, jt].astype(F32)
        m1 = mask_ref[t1, jt].astype(F32)
        parts.append(jnp.where(low, jnp.full((A, CH), m0, F32), jnp.full((A, CH), m1, F32)))
    return jnp.concatenate(parts, axis=0)


def rows_of(chunk):
    return pl.ds(pl.multiple_of(chunk * CHUNK, CHUNK), CHUNK)


def load_turned(ref, b0):
    return jnp.concatenate([ref[pl.ds(b0 + k, A, stride=B), :] for k in range(NB)], axis=0)


def store_turned(ref, b0, value):
    for k in range(NB):
        ref[pl.ds(b0 + k, A, stride=B), :] = value[k * A:(k + 1) * A]


def pack_two(ref, i, left, right):
    parts = []
    for k in range(NB):
        parts += [left[k * A:(k + 1) * A], right[k * A:(k + 1) * A]]
    items = jnp.concatenate(parts, axis=0)
    for t in range(6):
        ref[pl.ds(i * 6 + t, CH, stride=TWO_ROWS), :] = jnp.transpose(items[t * 128:(t + 1) * 128])


def unpack_two(wide, i):
    items = jnp.concatenate(
        [jnp.transpose(wide[pl.ds(i * 6 + t, CH, stride=TWO_ROWS), :]) for t in range(6)], axis=0
    )
    lefts = [items[k * 2 * A:k * 2 * A + A] for k in range(NB)]
    rights = [items[k * 2 * A + A:(k + 1) * 2 * A] for k in range(NB)]
    return jnp.concatenate(lefts, axis=0), jnp.concatenate(rights, axis=0)


def pack_one(ref, i, value):
    for t in range(3):
        ref[pl.ds(i * 3 + t, CH, stride=ONE_ROWS), :] = jnp.transpose(value[t * 128:(t + 1) * 128])


def unpack_one(wide, i):
    return jnp.concatenate(
        [jnp.transpose(wide[pl.ds(i * 3 + t, CH, stride=ONE_ROWS), :]) for t in range(3)], axis=0
    )


def send_one(msg_ref, msgf):
    msgf[pl.ds(ONE_ROWS - 1, CH, stride=ONE_ROWS), :] = jnp.zeros((CH, CH), F32)
    msg_ref[...] = msgf[...].astype(BF16)


def chunks(fn):
    def step(i, carry):
        fn(i, i * NB)
        return carry

    lax.fori_loop(0, B // NB, step, 0)


def move(src, dst, sem):
    copy = pltpu.make_async_copy(src, dst, sem)
    copy.start()
    return copy


def average():
    return jnp.full((CH, CH), 1.0 / CH, BF16)


def normalize(values, short):
    center = values - mm(short, average())
    inv = lax.rsqrt(jnp.mean(center * center, axis=-1, keepdims=True) + EPS)
    return center * inv, inv


def centered(weight, gain_row):
    gain = jnp.transpose(jnp.broadcast_to(gain_row, (CH, CH)))
    scaled = weight.astype(F32) * jnp.concatenate([gain] * (weight.shape[1] // CH), axis=1)
    scaled = scaled - jnp.mean(scaled, axis=0, keepdims=True)
    high = scaled.astype(BF16)
    return high, (scaled - high.astype(F32)).astype(BF16)


def norm_back(standard, inv, scaled):
    return inv * (scaled - standard * jnp.mean(scaled * standard, axis=-1, keepdims=True))


def save_norm(refs, rows, standard, inv):
    refs[0][rows, :] = standard
    refs[1][rows, :] = jnp.broadcast_to(inv, standard.shape)


def open_gates(gate, proj, rows, gate_refs, fac_refs):
    sides = []
    for k in range(2):
        value = proj[:, 2 * k * CH:(2 * k + 1) * CH]
        sig = jax.nn.sigmoid(proj[:, (2 * k + 1) * CH:(2 * k + 2) * CH])
        factor = gate * sig
        side = factor * value
        fac_refs[2 * k][rows, :] = factor
        fac_refs[2 * k + 1][rows, :] = side * (1.0 - sig)
        sides.append(side)
    sig = jax.nn.sigmoid(proj[:, 4 * CH:])
    factor = gate * sig
    gate_refs[0][rows, :] = factor
    gate_refs[1][rows, :] = factor * (1.0 - sig)
    return sides


def k_first(far_mask_ref, pair_ref, win_ref, gin_ref, msg_ref, x_ref, *refs):
    norms, gates, facs = refs[:2], refs[2:4], refs[4:8]
    pair, win, gin, wide, msgf, mask_ref, sems = refs[8:]
    far = ((pair_ref, pair), (win_ref.at[0], win), (gin_ref, gin), (far_mask_ref, mask_ref))
    loads = [move(src, dst, sems.at[k]) for k, (src, dst) in enumerate(far)]
    loads[0].wait()
    wide[...] = pair[...].astype(F32)
    for copy in loads[1:]:
        copy.wait()

    def chunk(i, b0):
        rows = rows_of(i)
        x = load_turned(wide, b0)
        short = x.astype(BF16)
        x_ref[rows, :] = short
        standard, inv = normalize(x, short)
        save_norm(norms, rows, standard, inv)
        proj = mm((standard * gin[0:1, :]).astype(BF16), win[...])
        left, right = open_gates(gate_chunk(mask_ref, b0), proj, rows, gates, facs)
        pack_two(msgf, i, left, right)

    chunks(chunk)
    msg_ref[...] = msgf[...].astype(BF16)


def k_second(
    mask_ref, in_ref, x_ref, gsig_ref, slope_ref, win_ref, wout_ref, gin_ref, gout_ref,
    msg_ref, mid_ref, slope_out_ref, *refs
):
    norms0, norms1, gates, facs = refs[:2], refs[2:4], refs[4:6], refs[6:10]
    wide, msgf = refs[10:]
    wide[...] = in_ref[...].astype(F32)

    def chunk(i, b0):
        rows = rows_of(i)
        value = unpack_one(wide, i)
        standard, inv = normalize(value, value.astype(BF16))
        save_norm(norms0, rows, standard, inv)
        update = mm((standard * gout_ref[0:1, :]).astype(BF16), wout_ref[0])
        slope_out_ref[rows, :] = slope_ref[rows, :] * update
        middle = (x_ref[rows, :].astype(F32) + gsig_ref[rows, :] * update).astype(BF16)
        mid_ref[rows, :] = middle
        standard, inv = normalize(middle.astype(F32), middle)
        save_norm(norms1, rows, standard, inv)
        proj = mm((standard * gin_ref[1:2, :]).astype(BF16), win_ref[1])
        left, right = open_gates(gate_chunk(mask_ref, b0), proj, rows, gates, facs)
        pack_two(msgf, i, left, right)

    chunks(chunk)
    msg_ref[...] = msgf[...].astype(BF16)


def k_third(
    in_ref, mid_ref, gsig_ref, slope_ref, cot_ref, wout_ref, gout_ref,
    msg_ref, out_ref, cot_out_ref, dgate_ref, wide, cotf, outf, msgf, high, low,
):
    wide[...] = in_ref[...].astype(F32)
    cotf[...] = cot_ref[...].astype(F32)
    high[...], low[...] = centered(wout_ref[1], gout_ref[1:2, :])

    def chunk(i, b0):
        rows = rows_of(i)
        grad = load_turned(cotf, b0)
        cot_out_ref[rows, :] = grad.astype(BF16)
        gsig = gsig_ref[rows, :]
        d_update = (grad * gsig).astype(BF16)
        scaled = mm_nt(d_update, high[...]) + mm_nt(d_update, low[...])
        value = unpack_one(wide, i)
        standard, inv = normalize(value, value.astype(BF16))
        pack_one(msgf, i, norm_back(standard, inv, scaled))
        update = mm((standard * gout_ref[1:2, :]).astype(BF16), wout_ref[1])
        store_turned(outf, b0, mid_ref[rows, :].astype(F32) + gsig * update)
        dgate_ref[rows, :] = (grad * slope_ref[rows, :] * update).astype(BF16)

    chunks(chunk)
    out_ref[...] = outf[...].astype(BF16)
    send_one(msg_ref, msgf)


def bottom_back(d_left, d_right, dgate_ref, facs, norms, high, low, rows):
    d_proj = jnp.concatenate(
        [
            (d_left * facs[0][rows, :]).astype(BF16),
            (d_left * facs[1][rows, :]).astype(BF16),
            (d_right * facs[2][rows, :]).astype(BF16),
            (d_right * facs[3][rows, :]).astype(BF16),
            dgate_ref[rows, :],
        ],
        axis=1,
    )
    scaled = mm_nt(d_proj, high[...]) + mm_nt(d_proj, low[...])
    return norm_back(norms[0][rows, :], norms[1][rows, :], scaled)


def k_fourth(
    in_ref, cot_ref, dgate1_ref, f0, f1, f2, f3, n0, n1, gsig0_ref, slope0_ref, m0, m1,
    win_ref, wout_ref, gin_ref, gout_ref, msg_ref, grad_ref, dgate0_ref,
    wide, msgf, high, low, out_high, out_low,
):
    wide[...] = in_ref[...].astype(F32)
    high[...], low[...] = centered(win_ref[1], gin_ref[1:2, :])
    out_high[...], out_low[...] = centered(wout_ref[0], gout_ref[0:1, :])

    def chunk(i, b0):
        rows = rows_of(i)
        d_left, d_right = unpack_two(wide, i)
        grad = cot_ref[rows, :].astype(F32) + bottom_back(
            d_left, d_right, dgate1_ref, (f0, f1, f2, f3), (n0, n1), high, low, rows
        )
        grad_ref[rows, :] = grad
        dgate0_ref[rows, :] = (grad * slope0_ref[rows, :]).astype(BF16)
        d_update = (grad * gsig0_ref[rows, :]).astype(BF16)
        scaled = mm_nt(d_update, out_high[...]) + mm_nt(d_update, out_low[...])
        pack_one(msgf, i, norm_back(m0[rows, :], m1[rows, :], scaled))

    chunks(chunk)
    send_one(msg_ref, msgf)


def k_fifth(
    in_ref, grad_ref, dgate0_ref, f0, f1, f2, f3, n0, n1, win_ref, gin_ref, out_ref, wide, high, low
):
    wide[...] = in_ref[...].astype(F32)
    high[...], low[...] = centered(win_ref[0], gin_ref[0:1, :])

    def chunk(i, b0):
        rows = rows_of(i)
        d_left, d_right = unpack_two(wide, i)
        grad = grad_ref[rows, :] + bottom_back(
            d_left, d_right, dgate0_ref, (f0, f1, f2, f3), (n0, n1), high, low, rows
        )
        store_turned(out_ref, b0, grad)

    chunks(chunk)


def lanes(n):
    return lax.broadcasted_iota(jnp.int32, (n, 128), 1)


def turn(value, shift):
    shift = shift % 128
    return value if shift == 0 else pltpu.roll(value, shift, axis=1)


def thread(segments, lane):
    value = segments[-1][1]
    for (_, part), (end, _) in zip(reversed(segments[:-1]), reversed(segments[1:])):
        value = jnp.where(lane < end, part, value)
    return value


def inside(t):
    return [p for p in range(8) if p * A < (t + 1) * 128 and (p + 1) * A > t * 128]


def swap(load, n):
    lane = lanes(n)
    turned = []
    for d in range(8):
        tiles = []
        for t in range(3):
            parts = [(max(q * A - t * 128, 0), load((q + d) % 8, t)) for q in inside(t)]
            tiles.append(turn(thread(parts, lane), A * d))
        turned.append(tiles)
    for q in range(8):
        t0, off = divmod(q * A, 128)
        split = min(A, 128 - off)
        result = []
        for t in range(3):
            segments = []
            for p in inside(t):
                base = p * A - t * 128
                pieces = [(0, split, t0)] + ([(split, A, t0 + 1)] if split < A else [])
                for first, last, source in pieces:
                    if base + last > 0 and base + first < 128:
                        segments.append((max(base + first, 0), turned[(p - q) % 8][source]))
            result.append(thread(segments, lane))
        yield q, result


PART = 8


def narrow(tiles, dst):
    for t in range(3):
        dst[:, t * 128:(t + 1) * 128] = tiles[t * RES:(t + 1) * RES, :].astype(BF16)


def keep(tiles, value):
    for t in range(3):
        tiles[t * RES:(t + 1) * RES, :] = value[:, t * 128:(t + 1) * 128]


def join_two(x_ref, xf, lf, rf, lt, rt):
    xf[...] = x_ref[...].astype(F32)
    group = COLS * TWO_ROWS
    for n in range(0, 96, PART):
        def load(r, t):
            return xf[pl.ds(r * group + 3 * n + t, PART, stride=3), :]

        for p, tiles in swap(load, PART):
            dst = (lf, rf)[p % 2]
            for t in range(3):
                dst[pl.ds(t * RES + 4 * n + p // 2, PART, stride=4), :] = tiles[t]
    narrow(lf, lt)
    narrow(rf, rt)


def split_two(lf, rf, o_ref, of):
    group = COLS * TWO_ROWS
    for n in range(0, 96, PART):
        def load(p, t):
            return (lf, rf)[p % 2][pl.ds(t * RES + 4 * n + p // 2, PART, stride=4), :]

        for r, tiles in swap(load, PART):
            for t in range(3):
                of[pl.ds(r * group + 3 * n + t, PART, stride=3), :] = tiles[t]
    o_ref[...] = of[...].astype(BF16)


def join_one(x_ref, xf, df, dst):
    xf[...] = x_ref[...].astype(F32)
    group = COLS * ONE_ROWS
    for m in range(3):
        for c in range(0, COLS, PART):
            def load(r, t):
                return xf[pl.ds(r * group + c * ONE_ROWS + 3 * m + t, PART, stride=ONE_ROWS), :]

            for q, tiles in swap(load, PART):
                for t in range(3):
                    df[pl.ds(t * RES + c * B + 8 * m + q, PART, stride=B), :] = tiles[t]
    narrow(df, dst)


def split_one(value, o_ref, of):
    group = COLS * ONE_ROWS
    for m in range(3):
        for c in range(0, COLS, PART):
            def load(q, t):
                return value[pl.ds(t * RES + c * B + 8 * m + q, PART, stride=B), :]

            for r, tiles in swap(load, PART):
                for t in range(3):
                    of[pl.ds(r * group + c * ONE_ROWS + 3 * m + t, PART, stride=ONE_ROWS), :] = tiles[t]
    send_one(o_ref, of)


def m_forward(u, x_ref, o_ref, lt, rt, xf, lf, rf, prod, of):
    join_two(x_ref, xf, lf, rf, lt, rt)
    if u == 0:
        keep(prod, mm_tn(rt[...], lt[...]))
    else:
        keep(prod, mm_nt(rt[...], lt[...]))
    split_one(prod, o_ref, of)


def m_backward(u, x_ref, lt, rt, o_ref, xf, df, dt, prod_l, prod_r, of):
    join_one(x_ref, xf, df, dt)
    if u == 0:
        keep(prod_l, mm(rt[...], dt[...]))
        keep(prod_r, mm_nt(lt[...], dt[...]))
    else:
        keep(prod_l, mm_tn(dt[...], rt[...]))
        keep(prod_r, mm(dt[...], lt[...]))
    split_two(prod_l, prod_r, o_ref, of)


def shape(*dims, dtype=BF16):
    return jax.ShapeDtypeStruct(dims, dtype)


def call(fn, outs, scratch, name, smem=False, far=()):
    def run(*args):
        specs = [HB if k in far else VM for k in range(len(args))]
        args = [
            pltpu.with_memory_space_constraint(a, pltpu.HBM) if k in far else a
            for k, a in enumerate(args)
        ]
        if smem:
            specs[0] = SM
        return pl.pallas_call(
            fn,
            out_shape=outs,
            in_specs=specs,
            out_specs=[VM] * len(outs),
            scratch_shapes=scratch,
            compiler_params=pltpu.CompilerParams(vmem_limit_bytes=16 * 1024 * 1024),
            name=name,
        )(*args)

    return run


def exchange(message, rows):
    message = message.reshape(ROWS * COLS, rows // 2, 2, 128)
    return lax.all_to_all(message, AXES, 0, 0, tiled=True).reshape(ROWS * COLS * rows, 128)


TWO = (CH * TWO_ROWS, 128)
ONE = (CH * ONE_ROWS, 128)
PAIR = (PAIRS, CH)
FULL = (RES, RES)
TILED = (3 * RES, 128)
KEEP = shape(*PAIR)
WIDE = shape(*PAIR, dtype=F32)


def wide(dims):
    return pltpu.VMEM(dims, F32)


def body(pair_state, tile_mask, weight_in, weight_out, gain_in, gain_out, cotangent):
    w, wo, gi, go = weight_in, weight_out, gain_in, gain_out
    full = shape(*FULL)
    square = pltpu.VMEM((CH, CH), BF16)
    broad = pltpu.VMEM((CH, 5 * CH), BF16)
    forward = [wide(TWO), wide(TILED), wide(TILED), wide(TILED), wide(ONE)]
    backward = [wide(ONE), wide(TILED), pltpu.VMEM(FULL, BF16), wide(TILED), wide(TILED), wide(TWO)]
    msg, x, n0, n1, gsig0, slope0, *fac0 = call(
        k_first, (shape(*TWO), KEEP) + (WIDE,) * 8,
        [pltpu.VMEM(PAIR, BF16), broad, wide((2, CH)), wide(PAIR), wide(TWO),
         pltpu.SMEM((TILES, TILES), jnp.int32), DMA((4,))],
        "first", far=(0, 1, 2, 3),
    )(tile_mask, pair_state.reshape(PAIRS, CH), w, gi)
    norm_x = (n0, n1)
    msg = exchange(msg, TWO_ROWS)
    msg, lt0, rt0 = call(
        functools.partial(m_forward, 0), (shape(*ONE), full, full), forward, "product0"
    )(msg)
    msg = exchange(msg, ONE_ROWS)
    msg, middle, slope0, i0, i1, m0, m1, gsig1, slope1, *fac1 = call(
        k_second, (shape(*TWO), KEEP) + (WIDE,) * 11, [wide(ONE), wide(TWO)], "second", smem=True
    )(tile_mask, msg, x, gsig0, slope0, w, wo, gi, go)
    msg = exchange(msg, TWO_ROWS)
    msg, lt1, rt1 = call(
        functools.partial(m_forward, 1), (shape(*ONE), full, full), forward, "product1"
    )(msg)
    msg = exchange(msg, ONE_ROWS)
    msg, updated, cot, dgate1 = call(
        k_third, (shape(*ONE), KEEP, KEEP, KEEP),
        [wide(ONE), wide(PAIR), wide(PAIR), wide(ONE), square, square], "third",
    )(msg, middle, gsig1, slope1, cotangent.reshape(PAIRS, CH), wo, go)
    msg = exchange(msg, ONE_ROWS)
    (msg,) = call(functools.partial(m_backward, 1), (shape(*TWO),), backward, "back1")(msg, lt1, rt1)
    msg = exchange(msg, TWO_ROWS)
    msg, grad, dgate0 = call(
        k_fourth, (shape(*ONE), WIDE, KEEP),
        [wide(TWO), wide(ONE), broad, broad, square, square], "fourth",
    )(msg, cot, dgate1, *fac1, m0, m1, gsig0, slope0, i0, i1, w, wo, gi, go)
    msg = exchange(msg, ONE_ROWS)
    (msg,) = call(functools.partial(m_backward, 0), (shape(*TWO),), backward, "back0")(msg, lt0, rt0)
    msg = exchange(msg, TWO_ROWS)
    (pair_grad,) = call(k_fifth, (WIDE,), [wide(TWO), broad, broad], "fifth")(
        msg, grad, dgate0, *fac0, *norm_x, w, gi
    )
    return updated.reshape(A, B, CH), pair_grad.reshape(A, B, CH)


def solution(mesh):
    return jax.shard_map(
        body,
        mesh=mesh,
        in_specs=(P("row", "col", None), P(), P(), P(), P(), P(), P("row", "col", None)),
        out_specs=(P("row", "col", None), P("row", "col", None)),
        check_vma=False,
    )
```

time: 185 us -> 163 us (0.88)
  blocking collectives: 159 us -> 143 us
  local copies, waits for them, and re-layouts: 3.99 us -> 0.7 us
    all_to_all x8, blocking collectives: 159 us -> 143 us  [exchange(): lax.all_to_all(message, AXES, 0, 0, tiled=True)]
    unnamed x18 -> x12, local copies, waits for them, and re-layouts: 3.99 us -> 0.7 us
where the time goes in v2:
time: 163 us
  blocking collectives  143 us (88%)
  Pallas kernels  19.1 us (12%)
    all_to_all x8, blocking collectives, exchange(): lax.all_to_all(message, AXES, 0, 0, tiled=True)  143 us
    pallas_call x9, Pallas kernels, run(): pl.pallas_call(fn, out_shape=outs, in_specs=specs, out_specs=[VM] * len(o...  19.1 us

profile of v2, /device:TPU:1, one launch (start us, length us, event | category | flops | bytes accessed | tf_op | source)
XLA Modules:
  0.0 163.1 jit_solution(18197102647071813349)
XLA Ops:
  0.6 2.8 %first.1 = (bf16[2304,128]{1,0:T(8,128)(2,1)S(1)}, bf16[1152,128]{1,0:T(8,128)(2,1)S(1)}, f32[1152,128]{1,0:T(8,128)S(1)}, f32[1152,128]{1,0:T(8,128)S(1)}, f32[...) custom-call(s32[3,3]{1,0:T(4,128)} %mask_ref.1, ...), custom_call_target="tpu_custom_call" | custom-call | tf_op jit(solution)/shard_map/first/pallas_call | solution.py:446
  3.4 25.5 %all_to_all.40 = bf16[128,9,2,128]{3,2,1,0:T(2,128)(2,1)S(1)} all-to-all(bf16[128,9,2,128]{3,2,1,0:T(2,128)(2,1)S(1)} %bitcast.31), channel_id=1, replica_groups=mesh['row'=8,'col'=16] {'row','col'}, dimensions={0} | all-to-all | bytes 1179648 | tf_op jit(solution)/shard_map/all_to_all | solution.py:461
  29.0 1.0 product0.1
  30.0 0.0 copy-start
  30.0 0.0 copy-start.1
  30.0 0.0 copy-start.4
  30.0 16.0 %all_to_all.41 = bf16[128,5,2,128]{3,2,1,0:T(2,128)(2,1)S(1)} all-to-all(bf16[128,5,2,128]{3,2,1,0:T(2,128)(2,1)S(1)} %bitcast.34), channel_id=1, replica_groups=mesh['row'=8,'col'=16] {'row','col'}, dimensions={0} | all-to-all | bytes 655360 | tf_op jit(solution)/shard_map/all_to_all | solution.py:461
  46.0 0.0 copy-start.5
  46.0 0.0 copy-start.3
  46.0 0.0 copy-done
  46.0 0.0 copy-done.1
  46.0 0.0 copy-done.4
  46.0 0.7 copy-done.5
  46.7 0.0 copy-done.3
  46.7 3.5 %second.1 = (bf16[2304,128]{1,0:T(8,128)(2,1)S(1)}, bf16[1152,128]{1,0:T(8,128)(2,1)S(1)}, f32[1152,128]{1,0:T(8,128)S(1)}, f32[1152,128]{1,0:T(8,128)S(1)}, f32...) custom-call(s32[3,3]{1,0:T(4,128)S(1)} %copy-done.5, ...), custom_call_target="tpu_custom_call" | custom-call | tf_op jit(solution)/shard_map/second/pallas_call | solution.py:446
  50.2 17.9 %all_to_all.42 = bf16[128,9,2,128]{3,2,1,0:T(2,128)(2,1)S(1)} all-to-all(bf16[128,9,2,128]{3,2,1,0:T(2,128)(2,1)S(1)} %bitcast.30), channel_id=1, replica_groups=mesh['row'=8,'col'=16] {'row','col'}, dimensions={0} | all-to-all | bytes 1179648 | tf_op jit(solution)/shard_map/all_to_all | solution.py:461
  68.1 0.9 product1.1
  69.1 0.0 copy-start.2
  69.1 16.0 %all_to_all.43 = bf16[128,5,2,128]{3,2,1,0:T(2,128)(2,1)S(1)} all-to-all(bf16[128,5,2,128]{3,2,1,0:T(2,128)(2,1)S(1)} %bitcast.35), channel_id=1, replica_groups=mesh['row'=8,'col'=16] {'row','col'}, dimensions={0} | all-to-all | bytes 655360 | tf_op jit(solution)/shard_map/all_to_all | solution.py:461
  85.1 0.0 copy-done.2
  85.1 2.6 %third.1 = (bf16[1280,128]{1,0:T(8,128)(2,1)S(1)}, bf16[1152,128]{1,0:T(8,128)(2,1)}, bf16[1152,128]{1,0:T(8,128)(2,1)S(1)}, bf16[1152,128]{1,0:T(8,128)(2,1)S(1)}) custom-call(bf16[1280,128]{1,0:T(8,128)(2,1)S(1)} %bitcast.29, bf16[1152,128]{1,0:T(8,128)(2,1)S(1)} %get-tuple-element.45.mid_ref, f32[1152,128]{1,0:T(8,128)S(1)} %get-tuple-element.46.gsig_ref, ...), custom_call_target="tpu_custom_call" | custom-call | tf_op jit(solution)/shard_map/third/pallas_call | solution.py:446
  87.6 15.5 %all_to_all.44 = bf16[128,5,2,128]{3,2,1,0:T(2,128)(2,1)S(1)} all-to-all(bf16[128,5,2,128]{3,2,1,0:T(2,128)(2,1)S(1)} %bitcast.33), channel_id=1, replica_groups=mesh['row'=8,'col'=16] {'row','col'}, dimensions={0} | all-to-all | bytes 655360 | tf_op jit(solution)/shard_map/all_to_all | solution.py:461
  103.2 1.2 back1.1
  104.3 17.9 %all_to_all.45 = bf16[128,9,2,128]{3,2,1,0:T(2,128)(2,1)S(1)} all-to-all(bf16[128,9,2,128]{3,2,1,0:T(2,128)(2,1)S(1)} %bitcast.23), channel_id=1, replica_groups=mesh['row'=8,'col'=16] {'row','col'}, dimensions={0} | all-to-all | bytes 1179648 | tf_op jit(solution)/shard_map/all_to_all | solution.py:461
  122.3 3.2 %fourth.1 = (bf16[1280,128]{1,0:T(8,128)(2,1)S(1)}, f32[1152,128]{1,0:T(8,128)S(1)}, bf16[1152,128]{1,0:T(8,128)(2,1)S(1)}) custom-call(bf16[2304,128]{1,0:T(8,128)(2,1)S(1)} %bitcast.25, bf16[1152,128]{1,0:T(8,128)(2,1)S(1)} %get-tuple-element.52.cot_ref, bf16[1152,128]{1,0:T(8,128)(2,1)S(1)} %get-tuple-element.53.dgate1_ref, ...), custom_call_target="tpu_custom_call" | custom-call | tf_op jit(solution)/shard_map/fourth/pallas_call | solution.py:446
  125.5 15.8 %all_to_all.46 = bf16[128,5,2,128]{3,2,1,0:T(2,128)(2,1)S(1)} all-to-all(bf16[128,5,2,128]{3,2,1,0:T(2,128)(2,1)S(1)} %bitcast.32), channel_id=1, replica_groups=mesh['row'=8,'col'=16] {'row','col'}, dimensions={0} | all-to-all | bytes 655360 | tf_op jit(solution)/shard_map/all_to_all | solution.py:461
  141.3 1.1 back0.1
  142.4 17.9 %all_to_all.47 = bf16[128,9,2,128]{3,2,1,0:T(2,128)(2,1)S(1)} all-to-all(bf16[128,9,2,128]{3,2,1,0:T(2,128)(2,1)S(1)} %bitcast.24), channel_id=1, replica_groups=mesh['row'=8,'col'=16] {'row','col'}, dimensions={0} | all-to-all | bytes 1179648 | tf_op jit(solution)/shard_map/all_to_all | solution.py:461
  160.4 2.8 %fifth.1 = f32[1152,128]{1,0:T(8,128)} custom-call(bf16[2304,128]{1,0:T(8,128)(2,1)S(1)} %bitcast.20, f32[1152,128]{1,0:T(8,128)S(1)} %get-tuple-element.66.grad_ref, bf16[1152,128]{1,0:T(8,128)(2,1)S(1)} %get-tuple-element.67.dgate0_ref, f32[1152,128]{1,0:T(8,128)S(1)} %get-tuple-element.68.f0, f32[1152,128]{1,0:T(8,128)S(1)} %get-tuple-element.69.f1, ...), custom_call_target="tpu_custom_call" | custom-call | tf_op jit(solution)/shard_map/fifth/pallas_call | solution.py:446
Async XLA Ops:
  30.0 16.0 %copy-start = (bf16[2,128,640]{2,1,0:T(8,128)(2,1)S(1)}, bf16[2,128,640]{2,1,0:T(8,128)(2,1)}, u32[]{:S(2)}) copy-start(bf16[2,128,640]{2,1,0:T(8,128)(2,1)} %win_ref.7) | copy-start | bytes 983044
  30.0 16.0 %copy-start.1 = (bf16[2,128,128]{2,1,0:T(8,128)(2,1)S(1)}, bf16[2,128,128]{2,1,0:T(8,128)(2,1)}, u32[]{:S(2)}) copy-start(bf16[2,128,128]{2,1,0:T(8,128)(2,1)} %wout_ref.5) | copy-start | bytes 196612
  30.0 16.0 %copy-start.4 = (f32[2,128]{1,0:T(2,128)S(1)}, f32[2,128]{1,0:T(2,128)}, u32[]{:S(2)}) copy-start(f32[2,128]{1,0:T(2,128)} %gout_ref.5) | copy-start | bytes 3076
  46.0 0.7 copy-start.5
  46.0 0.7 copy-start.3
  69.1 16.0 %copy-start.2 = (bf16[48,24,128]{2,1,0:T(8,128)(2,1)S(1)}, bf16[48,24,128]{2,1,0:T(8,128)(2,1)}, u32[]{:S(2)}) copy-start(bf16[48,24,128]{2,1,0:T(8,128)(2,1)} %param.13) | copy-start | bytes 884740

commit v3 on v2

--- a/solution.py
+++ b/solution.py
@@ -16,14 +16,13 @@
 A = RES // ROWS
 B = RES // COLS
 PAIRS = A * B
-NB = 8
+NB = 24
 CHUNK = NB * A
 F32 = jnp.float32
 BF16 = jnp.bfloat16
 EPS = 1e-05
 AXES = ("row", "col")
 VM = pl.BlockSpec(memory_space=pltpu.VMEM)
-SM = pl.BlockSpec(memory_space=pltpu.SMEM)
 HB = pl.BlockSpec(memory_space=pltpu.HBM)
 DMA = pltpu.SemaphoreType.DMA
 TWO_ROWS = 18
@@ -57,8 +56,8 @@
     return jnp.concatenate(parts, axis=0)
 
 
-def rows_of(chunk):
-    return pl.ds(pl.multiple_of(chunk * CHUNK, CHUNK), CHUNK)
+def rows_of(chunk, nb=NB):
+    return pl.ds(chunk * nb * A, nb * A)
 
 
 def load_turned(ref, b0):
@@ -75,27 +74,30 @@
     for k in range(NB):
         parts += [left[k * A:(k + 1) * A], right[k * A:(k + 1) * A]]
     items = jnp.concatenate(parts, axis=0)
-    for t in range(6):
-        ref[pl.ds(i * 6 + t, CH, stride=TWO_ROWS), :] = jnp.transpose(items[t * 128:(t + 1) * 128])
-
-
-def unpack_two(wide, i):
+    for t in range(NB * 2 * A // 128):
+        ref[pl.ds(i * (NB * 2 * A // 128) + t, CH, stride=TWO_ROWS), :] = jnp.transpose(items[t * 128:(t + 1) * 128])
+
+
+def unpack_two(wide, i, nb=NB):
+    blocks = nb * 2 * A // 128
     items = jnp.concatenate(
-        [jnp.transpose(wide[pl.ds(i * 6 + t, CH, stride=TWO_ROWS), :]) for t in range(6)], axis=0
+        [jnp.transpose(wide[pl.ds(i * blocks + t, CH, stride=TWO_ROWS), :]) for t in range(blocks)],
+        axis=0,
     )
-    lefts = [items[k * 2 * A:k * 2 * A + A] for k in range(NB)]
-    rights = [items[k * 2 * A + A:(k + 1) * 2 * A] for k in range(NB)]
+    lefts = [items[k * 2 * A:k * 2 * A + A] for k in range(nb)]
+    rights = [items[k * 2 * A + A:(k + 1) * 2 * A] for k in range(nb)]
     return jnp.concatenate(lefts, axis=0), jnp.concatenate(rights, axis=0)
 
 
 def pack_one(ref, i, value):
-    for t in range(3):
-        ref[pl.ds(i * 3 + t, CH, stride=ONE_ROWS), :] = jnp.transpose(value[t * 128:(t + 1) * 128])
+    for t in range(NB * A // 128):
+        ref[pl.ds(i * (NB * A // 128) + t, CH, stride=ONE_ROWS), :] = jnp.transpose(value[t * 128:(t + 1) * 128])
 
 
 def unpack_one(wide, i):
     return jnp.concatenate(
-        [jnp.transpose(wide[pl.ds(i * 3 + t, CH, stride=ONE_ROWS), :]) for t in range(3)], axis=0
+        [jnp.transpose(wide[pl.ds(i * (NB * A // 128) + t, CH, stride=ONE_ROWS), :])
+         for t in range(NB * A // 128)], axis=0
     )
 
 
@@ -105,11 +107,8 @@
 
 
 def chunks(fn):
-    def step(i, carry):
+    for i in range(B // NB):
         fn(i, i * NB)
-        return carry
-
-    lax.fori_loop(0, B // NB, step, 0)
 
 
 def move(src, dst, sem):
@@ -133,7 +132,12 @@
     scaled = weight.astype(F32) * jnp.concatenate([gain] * (weight.shape[1] // CH), axis=1)
     scaled = scaled - jnp.mean(scaled, axis=0, keepdims=True)
     high = scaled.astype(BF16)
-    return high, (scaled - high.astype(F32)).astype(BF16)
+    return jnp.concatenate([high, (scaled - high.astype(F32)).astype(BF16)], axis=0)
+
+
+def mm_centered(value, weight):
+    both = mm_nt(value, weight)
+    return both[:, :CH] + both[:, CH:]
 
 
 def norm_back(standard, inv, scaled):
@@ -162,7 +166,7 @@
     return sides
 
 
-def k_first(far_mask_ref, pair_ref, win_ref, gin_ref, msg_ref, x_ref, *refs):
+def k_first(far_mask_ref, pair_ref, win_ref, gin_ref, msg_ref, x_ref, gate_ref, gain_ref, *refs):
     norms, gates, facs = refs[:2], refs[2:4], refs[4:8]
     pair, win, gin, wide, msgf, mask_ref, sems = refs[8:]
     far = ((pair_ref, pair), (win_ref.at[0], win), (gin_ref, gin), (far_mask_ref, mask_ref))
@@ -171,6 +175,7 @@
     wide[...] = pair[...].astype(F32)
     for copy in loads[1:]:
         copy.wait()
+    gain_ref[...] = gin[...]
 
     def chunk(i, b0):
         rows = rows_of(i)
@@ -180,7 +185,9 @@
         standard, inv = normalize(x, short)
         save_norm(norms, rows, standard, inv)
         proj = mm((standard * gin[0:1, :]).astype(BF16), win[...])
-        left, right = open_gates(gate_chunk(mask_ref, b0), proj, rows, gates, facs)
+        gate = gate_chunk(mask_ref, b0)
+        gate_ref[rows, :] = gate
+        left, right = open_gates(gate, proj, rows, gates, facs)
         pack_two(msgf, i, left, right)
 
     chunks(chunk)
@@ -188,7 +195,7 @@
 
 
 def k_second(
-    mask_ref, in_ref, x_ref, gsig_ref, slope_ref, win_ref, wout_ref, gin_ref, gout_ref,
+    gate_ref, in_ref, x_ref, gsig_ref, slope_ref, win_ref, wout_ref, gin_ref, gout_ref,
     msg_ref, mid_ref, slope_out_ref, *refs
 ):
     norms0, norms1, gates, facs = refs[:2], refs[2:4], refs[4:6], refs[6:10]
@@ -207,7 +214,7 @@
         standard, inv = normalize(middle.astype(F32), middle)
         save_norm(norms1, rows, standard, inv)
         proj = mm((standard * gin_ref[1:2, :]).astype(BF16), win_ref[1])
-        left, right = open_gates(gate_chunk(mask_ref, b0), proj, rows, gates, facs)
+        left, right = open_gates(gate_ref[rows, :], proj, rows, gates, facs)
         pack_two(msgf, i, left, right)
 
     chunks(chunk)
@@ -216,11 +223,11 @@
 
 def k_third(
     in_ref, mid_ref, gsig_ref, slope_ref, cot_ref, wout_ref, gout_ref,
-    msg_ref, out_ref, cot_out_ref, dgate_ref, wide, cotf, outf, msgf, high, low,
+    msg_ref, out_ref, cot_out_ref, dgate_ref, wide, cotf, outf, msgf, back, out, sems,
 ):
     wide[...] = in_ref[...].astype(F32)
     cotf[...] = cot_ref[...].astype(F32)
-    high[...], low[...] = centered(wout_ref[1], gout_ref[1:2, :])
+    back[...] = centered(wout_ref[1], gout_ref[1:2, :])
 
     def chunk(i, b0):
         rows = rows_of(i)
@@ -228,20 +235,23 @@
         cot_out_ref[rows, :] = grad.astype(BF16)
         gsig = gsig_ref[rows, :]
         d_update = (grad * gsig).astype(BF16)
-        scaled = mm_nt(d_update, high[...]) + mm_nt(d_update, low[...])
+        scaled = mm_centered(d_update, back[...])
         value = unpack_one(wide, i)
         standard, inv = normalize(value, value.astype(BF16))
-        pack_one(msgf, i, norm_back(standard, inv, scaled))
         update = mm((standard * gout_ref[1:2, :]).astype(BF16), wout_ref[1])
         store_turned(outf, b0, mid_ref[rows, :].astype(F32) + gsig * update)
+        out[...] = outf[...].astype(BF16)
+        saves.append(move(out, out_ref, sems.at[0]))
         dgate_ref[rows, :] = (grad * slope_ref[rows, :] * update).astype(BF16)
-
+        pack_one(msgf, i, norm_back(standard, inv, scaled))
+
+    saves = []
     chunks(chunk)
-    out_ref[...] = outf[...].astype(BF16)
     send_one(msg_ref, msgf)
-
-
-def bottom_back(d_left, d_right, dgate_ref, facs, norms, high, low, rows):
+    saves[0].wait()
+
+
+def bottom_back(d_left, d_right, dgate_ref, facs, norms, back, rows):
     d_proj = jnp.concatenate(
         [
             (d_left * facs[0][rows, :]).astype(BF16),
@@ -252,50 +262,56 @@
         ],
         axis=1,
     )
-    scaled = mm_nt(d_proj, high[...]) + mm_nt(d_proj, low[...])
-    return norm_back(norms[0][rows, :], norms[1][rows, :], scaled)
+    return norm_back(norms[0][rows, :], norms[1][rows, :], mm_centered(d_proj, back[...]))
 
 
 def k_fourth(
     in_ref, cot_ref, dgate1_ref, f0, f1, f2, f3, n0, n1, gsig0_ref, slope0_ref, m0, m1,
     win_ref, wout_ref, gin_ref, gout_ref, msg_ref, grad_ref, dgate0_ref,
-    wide, msgf, high, low, out_high, out_low,
+    wide, msgf, back, out_back,
 ):
     wide[...] = in_ref[...].astype(F32)
-    high[...], low[...] = centered(win_ref[1], gin_ref[1:2, :])
-    out_high[...], out_low[...] = centered(wout_ref[0], gout_ref[0:1, :])
+    back[...] = centered(win_ref[1], gin_ref[1:2, :])
+    out_back[...] = centered(wout_ref[0], gout_ref[0:1, :])
 
     def chunk(i, b0):
         rows = rows_of(i)
         d_left, d_right = unpack_two(wide, i)
         grad = cot_ref[rows, :].astype(F32) + bottom_back(
-            d_left, d_right, dgate1_ref, (f0, f1, f2, f3), (n0, n1), high, low, rows
+            d_left, d_right, dgate1_ref, (f0, f1, f2, f3), (n0, n1), back, rows
         )
         grad_ref[rows, :] = grad
         dgate0_ref[rows, :] = (grad * slope0_ref[rows, :]).astype(BF16)
         d_update = (grad * gsig0_ref[rows, :]).astype(BF16)
-        scaled = mm_nt(d_update, out_high[...]) + mm_nt(d_update, out_low[...])
+        scaled = mm_centered(d_update, out_back[...])
         pack_one(msgf, i, norm_back(m0[rows, :], m1[rows, :], scaled))
 
     chunks(chunk)
     send_one(msg_ref, msgf)
 
 
+PIECE = 8
+
+
 def k_fifth(
-    in_ref, grad_ref, dgate0_ref, f0, f1, f2, f3, n0, n1, win_ref, gin_ref, out_ref, wide, high, low
+    in_ref, grad_ref, dgate0_ref, f0, f1, f2, f3, n0, n1, win_ref, gin_ref, out_ref,
+    wide, back, outf, sems,
 ):
     wide[...] = in_ref[...].astype(F32)
-    high[...], low[...] = centered(win_ref[0], gin_ref[0:1, :])
-
-    def chunk(i, b0):
-        rows = rows_of(i)
-        d_left, d_right = unpack_two(wide, i)
+    back[...] = centered(win_ref[0], gin_ref[0:1, :])
+    saves = []
+    for i in range(B // PIECE):
+        rows = rows_of(i, PIECE)
+        d_left, d_right = unpack_two(wide, i, PIECE)
         grad = grad_ref[rows, :] + bottom_back(
-            d_left, d_right, dgate0_ref, (f0, f1, f2, f3), (n0, n1), high, low, rows
+            d_left, d_right, dgate0_ref, (f0, f1, f2, f3), (n0, n1), back, rows
         )
-        store_turned(out_ref, b0, grad)
-
-    chunks(chunk)
+        for k in range(PIECE):
+            outf[pl.ds(i * PIECE + k, A, stride=B), :] = grad[k * A:(k + 1) * A]
+        part = pl.ds(i * PIECE, PIECE)
+        saves.append(move(outf.reshape(A, B, CH).at[:, part, :], out_ref.at[:, part, :], sems.at[i]))
+    for copy in saves:
+        copy.wait()
 
 
 def lanes(n):
@@ -434,20 +450,18 @@
     return jax.ShapeDtypeStruct(dims, dtype)
 
 
-def call(fn, outs, scratch, name, smem=False, far=()):
+def call(fn, outs, scratch, name, far=(), far_out=()):
     def run(*args):
         specs = [HB if k in far else VM for k in range(len(args))]
         args = [
             pltpu.with_memory_space_constraint(a, pltpu.HBM) if k in far else a
             for k, a in enumerate(args)
         ]
-        if smem:
-            specs[0] = SM
         return pl.pallas_call(
             fn,
             out_shape=outs,
             in_specs=specs,
-            out_specs=[VM] * len(outs),
+            out_specs=[HB if k in far_out else VM for k in range(len(outs))],
             scratch_shapes=scratch,
             compiler_params=pltpu.CompilerParams(vmem_limit_bytes=16 * 1024 * 1024),
             name=name,
@@ -477,13 +491,13 @@
 def body(pair_state, tile_mask, weight_in, weight_out, gain_in, gain_out, cotangent):
     w, wo, gi, go = weight_in, weight_out, gain_in, gain_out
     full = shape(*FULL)
-    square = pltpu.VMEM((CH, CH), BF16)
-    broad = pltpu.VMEM((CH, 5 * CH), BF16)
+    square = pltpu.VMEM((2 * CH, CH), BF16)
+    broad = pltpu.VMEM((2 * CH, 5 * CH), BF16)
     forward = [wide(TWO), wide(TILED), wide(TILED), wide(TILED), wide(ONE)]
     backward = [wide(ONE), wide(TILED), pltpu.VMEM(FULL, BF16), wide(TILED), wide(TILED), wide(TWO)]
-    msg, x, n0, n1, gsig0, slope0, *fac0 = call(
-        k_first, (shape(*TWO), KEEP) + (WIDE,) * 8,
-        [pltpu.VMEM(PAIR, BF16), broad, wide((2, CH)), wide(PAIR), wide(TWO),
+    msg, x, gate, gi, n0, n1, gsig0, slope0, *fac0 = call(
+        k_first, (shape(*TWO), KEEP, WIDE, shape(2, CH, dtype=F32)) + (WIDE,) * 8,
+        [pltpu.VMEM(PAIR, BF16), pltpu.VMEM((CH, 5 * CH), BF16), wide((2, CH)), wide(PAIR), wide(TWO),
          pltpu.SMEM((TILES, TILES), jnp.int32), DMA((4,))],
         "first", far=(0, 1, 2, 3),
     )(tile_mask, pair_state.reshape(PAIRS, CH), w, gi)
@@ -494,31 +508,33 @@
     )(msg)
     msg = exchange(msg, ONE_ROWS)
     msg, middle, slope0, i0, i1, m0, m1, gsig1, slope1, *fac1 = call(
-        k_second, (shape(*TWO), KEEP) + (WIDE,) * 11, [wide(ONE), wide(TWO)], "second", smem=True
-    )(tile_mask, msg, x, gsig0, slope0, w, wo, gi, go)
+        k_second, (shape(*TWO), KEEP) + (WIDE,) * 11, [wide(ONE), wide(TWO)], "second"
+    )(gate, msg, x, gsig0, slope0, w, wo, gi, go)
     msg = exchange(msg, TWO_ROWS)
     msg, lt1, rt1 = call(
         functools.partial(m_forward, 1), (shape(*ONE), full, full), forward, "product1"
     )(msg)
     msg = exchange(msg, ONE_ROWS)
     msg, updated, cot, dgate1 = call(
-        k_third, (shape(*ONE), KEEP, KEEP, KEEP),
-        [wide(ONE), wide(PAIR), wide(PAIR), wide(ONE), square, square], "third",
+        k_third, (shape(*ONE), pltpu.HBM(PAIR, BF16), KEEP, KEEP),
+        [wide(ONE), wide(PAIR), wide(PAIR), wide(ONE), square,
+         pltpu.VMEM(PAIR, BF16), DMA((1,))], "third", far_out=(1,),
     )(msg, middle, gsig1, slope1, cotangent.reshape(PAIRS, CH), wo, go)
     msg = exchange(msg, ONE_ROWS)
     (msg,) = call(functools.partial(m_backward, 1), (shape(*TWO),), backward, "back1")(msg, lt1, rt1)
     msg = exchange(msg, TWO_ROWS)
     msg, grad, dgate0 = call(
         k_fourth, (shape(*ONE), WIDE, KEEP),
-        [wide(TWO), wide(ONE), broad, broad, square, square], "fourth",
+        [wide(TWO), wide(ONE), broad, square], "fourth",
     )(msg, cot, dgate1, *fac1, m0, m1, gsig0, slope0, i0, i1, w, wo, gi, go)
     msg = exchange(msg, ONE_ROWS)
     (msg,) = call(functools.partial(m_backward, 0), (shape(*TWO),), backward, "back0")(msg, lt0, rt0)
     msg = exchange(msg, TWO_ROWS)
-    (pair_grad,) = call(k_fifth, (WIDE,), [wide(TWO), broad, broad], "fifth")(
-        msg, grad, dgate0, *fac0, *norm_x, w, gi
-    )
-    return updated.reshape(A, B, CH), pair_grad.reshape(A, B, CH)
+    (pair_grad,) = call(
+        k_fifth, (pltpu.HBM((A, B, CH), F32),),
+        [wide(TWO), broad, wide(PAIR), DMA((B // PIECE,))], "fifth", far_out=(0,),
+    )(msg, grad, dgate0, *fac0, *norm_x, w, gi)
+    return updated.reshape(A, B, CH), pair_grad
 
 
 def solution(mesh):

time: 163 us -> 157 us (0.963)
  Pallas kernels: 19.1 us -> 12.5 us
    pallas_call x9, Pallas kernels: 19.1 us -> 12.5 us  [run(): pl.pallas_call(fn, out_shape=outs, in_specs=specs, out_specs=[HB if k in...]
where the time goes in v3:
time: 157 us
  blocking collectives  143 us (91%)
  Pallas kernels  12.5 us (8%)
    all_to_all x8, blocking collectives, exchange(): lax.all_to_all(message, AXES, 0, 0, tiled=True)  143 us
    pallas_call x9, Pallas kernels, run(): pl.pallas_call(fn, out_shape=outs, in_specs=specs, out_specs=[HB if k in...  12.5 us

profile of v3, /device:TPU:1, one launch (start us, length us, event | category | flops | bytes accessed | tf_op | source)
XLA Modules:
  0.0 156.9 jit_solution(5747041770664299786)
XLA Ops:
  0.6 1.9 %first.1 = (bf16[2304,128]{1,0:T(8,128)(2,1)S(1)}, bf16[1152,128]{1,0:T(8,128)(2,1)S(1)}, f32[1152,128]{1,0:T(8,128)S(1)}, f32[2,128]{1,0:T(2,128)S(1)}, f32[115...) custom-call(s32[3,3]{1,0:T(4,128)} %far_mask_ref.1, ...), custom_call_target="tpu_custom_call" | custom-call | tf_op jit(solution)/shard_map/first/pallas_call | solution.py:460
  2.6 25.5 %all_to_all.40 = bf16[128,9,2,128]{3,2,1,0:T(2,128)(2,1)S(1)} all-to-all(bf16[128,9,2,128]{3,2,1,0:T(2,128)(2,1)S(1)} %bitcast.30), channel_id=1, replica_groups=mesh['row'=8,'col'=16] {'row','col'}, dimensions={0} | all-to-all | bytes 1179648 | tf_op jit(solution)/shard_map/all_to_all | solution.py:475
  28.1 1.0 product0.1
  29.2 0.0 copy-start
  29.2 0.0 copy-start.1
  29.2 16.0 %all_to_all.41 = bf16[128,5,2,128]{3,2,1,0:T(2,128)(2,1)S(1)} all-to-all(bf16[128,5,2,128]{3,2,1,0:T(2,128)(2,1)S(1)} %bitcast.33), channel_id=1, replica_groups=mesh['row'=8,'col'=16] {'row','col'}, dimensions={0} | all-to-all | bytes 655360 | tf_op jit(solution)/shard_map/all_to_all | solution.py:475
  45.1 0.0 copy-start.3
  45.2 0.0 copy-done
  45.2 0.0 copy-done.1
  45.2 0.7 copy-done.3
  45.8 1.4 second.1
  47.2 17.9 %all_to_all.42 = bf16[128,9,2,128]{3,2,1,0:T(2,128)(2,1)S(1)} all-to-all(bf16[128,9,2,128]{3,2,1,0:T(2,128)(2,1)S(1)} %bitcast.29), channel_id=1, replica_groups=mesh['row'=8,'col'=16] {'row','col'}, dimensions={0} | all-to-all | bytes 1179648 | tf_op jit(solution)/shard_map/all_to_all | solution.py:475
  65.2 0.9 product1.1
  66.1 0.0 copy-start.2
  66.1 16.0 %all_to_all.43 = bf16[128,5,2,128]{3,2,1,0:T(2,128)(2,1)S(1)} all-to-all(bf16[128,5,2,128]{3,2,1,0:T(2,128)(2,1)S(1)} %bitcast.34), channel_id=1, replica_groups=mesh['row'=8,'col'=16] {'row','col'}, dimensions={0} | all-to-all | bytes 655360 | tf_op jit(solution)/shard_map/all_to_all | solution.py:475
  82.1 0.0 copy-done.2
  82.1 1.6 %third.1 = (bf16[1280,128]{1,0:T(8,128)(2,1)S(1)}, bf16[1152,128]{1,0:T(8,128)(2,1)}, bf16[1152,128]{1,0:T(8,128)(2,1)S(1)}, bf16[1152,128]{1,0:T(8,128)(2,1)S(1)}) custom-call(bf16[1280,128]{1,0:T(8,128)(2,1)S(1)} %bitcast.28, bf16[1152,128]{1,0:T(8,128)(2,1)S(1)} %get-tuple-element.49.mid_ref, f32[1152,128]{1,0:T(8,128)S(1)} %get-tuple-element.50.gsig_ref, ...), custom_call_target="tpu_custom_call" | custom-call | tf_op jit(solution)/shard_map/third/pallas_call | solution.py:460
  83.7 15.5 %all_to_all.44 = bf16[128,5,2,128]{3,2,1,0:T(2,128)(2,1)S(1)} all-to-all(bf16[128,5,2,128]{3,2,1,0:T(2,128)(2,1)S(1)} %bitcast.32), channel_id=1, replica_groups=mesh['row'=8,'col'=16] {'row','col'}, dimensions={0} | all-to-all | bytes 655360 | tf_op jit(solution)/shard_map/all_to_all | solution.py:475
  99.3 1.2 back1.1
  100.4 17.9 %all_to_all.45 = bf16[128,9,2,128]{3,2,1,0:T(2,128)(2,1)S(1)} all-to-all(bf16[128,9,2,128]{3,2,1,0:T(2,128)(2,1)S(1)} %bitcast.22), channel_id=1, replica_groups=mesh['row'=8,'col'=16] {'row','col'}, dimensions={0} | all-to-all | bytes 1179648 | tf_op jit(solution)/shard_map/all_to_all | solution.py:475
  118.4 1.6 %fourth.1 = (bf16[1280,128]{1,0:T(8,128)(2,1)S(1)}, f32[1152,128]{1,0:T(8,128)S(1)}, bf16[1152,128]{1,0:T(8,128)(2,1)S(1)}) custom-call(bf16[2304,128]{1,0:T(8,128)(2,1)S(1)} %bitcast.24, bf16[1152,128]{1,0:T(8,128)(2,1)S(1)} %get-tuple-element.56.cot_ref, bf16[1152,128]{1,0:T(8,128)(2,1)S(1)} %get-tuple-element.57.dgate1_ref, ...), custom_call_target="tpu_custom_call" | custom-call | tf_op jit(solution)/shard_map/fourth/pallas_call | solution.py:460
  120.0 16.0 %all_to_all.46 = bf16[128,5,2,128]{3,2,1,0:T(2,128)(2,1)S(1)} all-to-all(bf16[128,5,2,128]{3,2,1,0:T(2,128)(2,1)S(1)} %bitcast.31), channel_id=1, replica_groups=mesh['row'=8,'col'=16] {'row','col'}, dimensions={0} | all-to-all | bytes 655360 | tf_op jit(solution)/shard_map/all_to_all | solution.py:475
  136.0 1.1 back0.1
  137.1 17.9 %all_to_all.47 = bf16[128,9,2,128]{3,2,1,0:T(2,128)(2,1)S(1)} all-to-all(bf16[128,9,2,128]{3,2,1,0:T(2,128)(2,1)S(1)} %bitcast.23), channel_id=1, replica_groups=mesh['row'=8,'col'=16] {'row','col'}, dimensions={0} | all-to-all | bytes 1179648 | tf_op jit(solution)/shard_map/all_to_all | solution.py:475
  155.0 1.7 %fifth.1 = f32[48,24,128]{2,1,0:T(8,128)} custom-call(bf16[2304,128]{1,0:T(8,128)(2,1)S(1)} %bitcast.19, f32[1152,128]{1,0:T(8,128)S(1)} %get-tuple-element.70.grad_ref, bf16[1152,128]{1,0:T(8,128)(2,1)S(1)} %get-tuple-element.71.dgate0_ref, f32[1152,128]{1,0:T(8,128)S(1)} %get-tuple-element.72.f0, f32[1152,128]{1,0:T(8,128)S(1)} %get-tuple-element.73.f1, ...), custom_call_target="tpu_custom_call" | custom-call | tf_op jit(solution)/shard_map/fifth/pallas_call | solution.py:460
Async XLA Ops:
  29.2 16.0 %copy-start = (bf16[2,128,640]{2,1,0:T(8,128)(2,1)S(1)}, bf16[2,128,640]{2,1,0:T(8,128)(2,1)}, u32[]{:S(2)}) copy-start(bf16[2,128,640]{2,1,0:T(8,128)(2,1)} %win_ref.7) | copy-start | bytes 983044
  29.2 16.0 %copy-start.1 = (bf16[2,128,128]{2,1,0:T(8,128)(2,1)S(1)}, bf16[2,128,128]{2,1,0:T(8,128)(2,1)}, u32[]{:S(2)}) copy-start(bf16[2,128,128]{2,1,0:T(8,128)(2,1)} %wout_ref.5) | copy-start | bytes 196612
  45.1 0.7 copy-start.3
  66.1 16.0 %copy-start.2 = (bf16[48,24,128]{2,1,0:T(8,128)(2,1)S(1)}, bf16[48,24,128]{2,1,0:T(8,128)(2,1)}, u32[]{:S(2)}) copy-start(bf16[48,24,128]{2,1,0:T(8,128)(2,1)} %param.13) | copy-start | bytes 884740

commit v4 on v3

--- a/solution.py
+++ b/solution.py
@@ -166,15 +166,18 @@
     return sides
 
 
-def k_first(far_mask_ref, pair_ref, win_ref, gin_ref, msg_ref, x_ref, gate_ref, gain_ref, *refs):
+def k_first(
+    far_mask_ref, pair_ref, win_ref, gin_ref, gout_ref, msg_ref, x_ref, gate_ref, gain_ref, gain_out_ref, *refs
+):
     norms, gates, facs = refs[:2], refs[2:4], refs[4:8]
-    pair, win, gin, wide, msgf, mask_ref, sems = refs[8:]
-    far = ((pair_ref, pair), (win_ref.at[0], win), (gin_ref, gin), (far_mask_ref, mask_ref))
+    pair, win, gin, gout, wide, msgf, mask_ref, sems = refs[8:]
+    far = ((pair_ref, pair), (win_ref.at[0], win), (gin_ref, gin), (gout_ref, gout), (far_mask_ref, mask_ref))
     loads = [move(src, dst, sems.at[k]) for k, (src, dst) in enumerate(far)]
     loads[0].wait()
     wide[...] = pair[...].astype(F32)
     for copy in loads[1:]:
         copy.wait()
+    gain_out_ref[...] = gout[...]
     gain_ref[...] = gin[...]
 
     def chunk(i, b0):
@@ -223,7 +226,7 @@
 
 def k_third(
     in_ref, mid_ref, gsig_ref, slope_ref, cot_ref, wout_ref, gout_ref,
-    msg_ref, out_ref, cot_out_ref, dgate_ref, wide, cotf, outf, msgf, back, out, sems,
+    msg_ref, out_ref, cot_out_ref, dgate_ref, wide, cotf, outf, msgf, back,
 ):
     wide[...] = in_ref[...].astype(F32)
     cotf[...] = cot_ref[...].astype(F32)
@@ -240,15 +243,12 @@
         standard, inv = normalize(value, value.astype(BF16))
         update = mm((standard * gout_ref[1:2, :]).astype(BF16), wout_ref[1])
         store_turned(outf, b0, mid_ref[rows, :].astype(F32) + gsig * update)
-        out[...] = outf[...].astype(BF16)
-        saves.append(move(out, out_ref, sems.at[0]))
+        out_ref[...] = outf[...].astype(BF16)
         dgate_ref[rows, :] = (grad * slope_ref[rows, :] * update).astype(BF16)
         pack_one(msgf, i, norm_back(standard, inv, scaled))
 
-    saves = []
     chunks(chunk)
     send_one(msg_ref, msgf)
-    saves[0].wait()
 
 
 def bottom_back(d_left, d_right, dgate_ref, facs, norms, back, rows):
@@ -267,9 +267,10 @@
 
 def k_fourth(
     in_ref, cot_ref, dgate1_ref, f0, f1, f2, f3, n0, n1, gsig0_ref, slope0_ref, m0, m1,
-    win_ref, wout_ref, gin_ref, gout_ref, msg_ref, grad_ref, dgate0_ref,
-    wide, msgf, back, out_back,
+    win_ref, wout_ref, gin_ref, gout_ref, done_ref, msg_ref, grad_ref, dgate0_ref, far_done_ref,
+    wide, msgf, back, out_back, sems,
 ):
+    save = move(done_ref, far_done_ref, sems.at[0])
     wide[...] = in_ref[...].astype(F32)
     back[...] = centered(win_ref[1], gin_ref[1:2, :])
     out_back[...] = centered(wout_ref[0], gout_ref[0:1, :])
@@ -288,6 +289,7 @@
 
     chunks(chunk)
     send_one(msg_ref, msgf)
+    save.wait()
 
 
 PIECE = 8
@@ -495,12 +497,12 @@
     broad = pltpu.VMEM((2 * CH, 5 * CH), BF16)
     forward = [wide(TWO), wide(TILED), wide(TILED), wide(TILED), wide(ONE)]
     backward = [wide(ONE), wide(TILED), pltpu.VMEM(FULL, BF16), wide(TILED), wide(TILED), wide(TWO)]
-    msg, x, gate, gi, n0, n1, gsig0, slope0, *fac0 = call(
-        k_first, (shape(*TWO), KEEP, WIDE, shape(2, CH, dtype=F32)) + (WIDE,) * 8,
-        [pltpu.VMEM(PAIR, BF16), pltpu.VMEM((CH, 5 * CH), BF16), wide((2, CH)), wide(PAIR), wide(TWO),
-         pltpu.SMEM((TILES, TILES), jnp.int32), DMA((4,))],
-        "first", far=(0, 1, 2, 3),
-    )(tile_mask, pair_state.reshape(PAIRS, CH), w, gi)
+    msg, x, gate, gi, go, n0, n1, gsig0, slope0, *fac0 = call(
+        k_first, (shape(*TWO), KEEP, WIDE) + (shape(2, CH, dtype=F32),) * 2 + (WIDE,) * 8,
+        [pltpu.VMEM(PAIR, BF16), pltpu.VMEM((CH, 5 * CH), BF16), wide((2, CH)), wide((2, CH)),
+         wide(PAIR), wide(TWO), pltpu.SMEM((TILES, TILES), jnp.int32), DMA((5,))],
+        "first", far=(0, 1, 2, 3, 4),
+    )(tile_mask, pair_state.reshape(PAIRS, CH), w, gi, go)
     norm_x = (n0, n1)
     msg = exchange(msg, TWO_ROWS)
     msg, lt0, rt0 = call(
@@ -516,17 +518,16 @@
     )(msg)
     msg = exchange(msg, ONE_ROWS)
     msg, updated, cot, dgate1 = call(
-        k_third, (shape(*ONE), pltpu.HBM(PAIR, BF16), KEEP, KEEP),
-        [wide(ONE), wide(PAIR), wide(PAIR), wide(ONE), square,
-         pltpu.VMEM(PAIR, BF16), DMA((1,))], "third", far_out=(1,),
+        k_third, (shape(*ONE), KEEP, KEEP, KEEP),
+        [wide(ONE), wide(PAIR), wide(PAIR), wide(ONE), square], "third",
     )(msg, middle, gsig1, slope1, cotangent.reshape(PAIRS, CH), wo, go)
     msg = exchange(msg, ONE_ROWS)
     (msg,) = call(functools.partial(m_backward, 1), (shape(*TWO),), backward, "back1")(msg, lt1, rt1)
     msg = exchange(msg, TWO_ROWS)
-    msg, grad, dgate0 = call(
-        k_fourth, (shape(*ONE), WIDE, KEEP),
-        [wide(TWO), wide(ONE), broad, square], "fourth",
-    )(msg, cot, dgate1, *fac1, m0, m1, gsig0, slope0, i0, i1, w, wo, gi, go)
+    msg, grad, dgate0, updated = call(
+        k_fourth, (shape(*ONE), WIDE, KEEP, pltpu.HBM(PAIR, BF16)),
+        [wide(TWO), wide(ONE), broad, square, DMA((1,))], "fourth", far_out=(3,),
+    )(msg, cot, dgate1, *fac1, m0, m1, gsig0, slope0, i0, i1, w, wo, gi, go, updated)
     msg = exchange(msg, ONE_ROWS)
     (msg,) = call(functools.partial(m_backward, 0), (shape(*TWO),), backward, "back0")(msg, lt0, rt0)
     msg = exchange(msg, TWO_ROWS)

time: 157 us -> 156 us (level)
  no operation moved by 1% of the time
where the time goes in v4:
time: 156 us
  blocking collectives  143 us (92%)
  Pallas kernels  12.1 us (8%)
    all_to_all x8, blocking collectives, exchange(): lax.all_to_all(message, AXES, 0, 0, tiled=True)  143 us
    pallas_call x9, Pallas kernels, run(): pl.pallas_call(fn, out_shape=outs, in_specs=specs, out_specs=[HB if k in...  12.1 us

profile of v4, /device:TPU:1, one launch (start us, length us, event | category | flops | bytes accessed | tf_op | source)
XLA Modules:
  0.0 155.8 jit_solution(2458629922733675362)
XLA Ops:
  0.6 2.0 %first.1 = (bf16[2304,128]{1,0:T(8,128)(2,1)S(1)}, bf16[1152,128]{1,0:T(8,128)(2,1)S(1)}, f32[1152,128]{1,0:T(8,128)S(1)}, f32[2,128]{1,0:T(2,128)S(1)}, f32[2,1...) custom-call(s32[3,3]{1,0:T(4,128)} %far_mask_ref.1, ...), custom_call_target="tpu_custom_call" | custom-call | tf_op jit(solution)/shard_map/first/pallas_call | solution.py:462
  2.6 25.5 %all_to_all.40 = bf16[128,9,2,128]{3,2,1,0:T(2,128)(2,1)S(1)} all-to-all(bf16[128,9,2,128]{3,2,1,0:T(2,128)(2,1)S(1)} %bitcast.30), channel_id=1, replica_groups=mesh['row'=8,'col'=16] {'row','col'}, dimensions={0} | all-to-all | bytes 1179648 | tf_op jit(solution)/shard_map/all_to_all | solution.py:477
  28.1 1.0 product0.1
  29.2 0.0 copy-start
  29.2 0.0 copy-start.1
  29.2 16.0 %all_to_all.41 = bf16[128,5,2,128]{3,2,1,0:T(2,128)(2,1)S(1)} all-to-all(bf16[128,5,2,128]{3,2,1,0:T(2,128)(2,1)S(1)} %bitcast.33), channel_id=1, replica_groups=mesh['row'=8,'col'=16] {'row','col'}, dimensions={0} | all-to-all | bytes 655360 | tf_op jit(solution)/shard_map/all_to_all | solution.py:477
  45.2 0.0 copy-done
  45.2 0.0 copy-done.1
  45.2 1.4 second.1
  46.6 17.9 %all_to_all.42 = bf16[128,9,2,128]{3,2,1,0:T(2,128)(2,1)S(1)} all-to-all(bf16[128,9,2,128]{3,2,1,0:T(2,128)(2,1)S(1)} %bitcast.29), channel_id=1, replica_groups=mesh['row'=8,'col'=16] {'row','col'}, dimensions={0} | all-to-all | bytes 1179648 | tf_op jit(solution)/shard_map/all_to_all | solution.py:477
  64.5 0.9 product1.1
  65.5 0.0 copy-start.2
  65.5 16.0 %all_to_all.43 = bf16[128,5,2,128]{3,2,1,0:T(2,128)(2,1)S(1)} all-to-all(bf16[128,5,2,128]{3,2,1,0:T(2,128)(2,1)S(1)} %bitcast.34), channel_id=1, replica_groups=mesh['row'=8,'col'=16] {'row','col'}, dimensions={0} | all-to-all | bytes 655360 | tf_op jit(solution)/shard_map/all_to_all | solution.py:477
  81.4 0.0 copy-done.2
  81.4 1.2 third.1
  82.7 15.5 %all_to_all.44 = bf16[128,5,2,128]{3,2,1,0:T(2,128)(2,1)S(1)} all-to-all(bf16[128,5,2,128]{3,2,1,0:T(2,128)(2,1)S(1)} %bitcast.32), channel_id=1, replica_groups=mesh['row'=8,'col'=16] {'row','col'}, dimensions={0} | all-to-all | bytes 655360 | tf_op jit(solution)/shard_map/all_to_all | solution.py:477
  98.2 1.1 back1.1
  99.3 17.9 %all_to_all.45 = bf16[128,9,2,128]{3,2,1,0:T(2,128)(2,1)S(1)} all-to-all(bf16[128,9,2,128]{3,2,1,0:T(2,128)(2,1)S(1)} %bitcast.23), channel_id=1, replica_groups=mesh['row'=8,'col'=16] {'row','col'}, dimensions={0} | all-to-all | bytes 1179648 | tf_op jit(solution)/shard_map/all_to_all | solution.py:477
  117.3 1.6 %fourth.1 = (bf16[1280,128]{1,0:T(8,128)(2,1)S(1)}, f32[1152,128]{1,0:T(8,128)S(1)}, bf16[1152,128]{1,0:T(8,128)(2,1)S(1)}, bf16[1152,128]{1,0:T(8,128)(2,1)}) custom-call(bf16[2304,128]{1,0:T(8,128)(2,1)S(1)} %bitcast.19, bf16[1152,128]{1,0:T(8,128)(2,1)S(1)} %get-tuple-element.58.cot_ref, bf16[1152,128]{1,0:T(8,128)(2,1)S(1)} %get-tuple-element.59.dgate1_ref, ...), custom_call_target="tpu_custom_call" | custom-call | tf_op jit(solution)/shard_map/fourth/pallas_call | solution.py:462
  118.9 16.0 %all_to_all.46 = bf16[128,5,2,128]{3,2,1,0:T(2,128)(2,1)S(1)} all-to-all(bf16[128,5,2,128]{3,2,1,0:T(2,128)(2,1)S(1)} %bitcast.31), channel_id=1, replica_groups=mesh['row'=8,'col'=16] {'row','col'}, dimensions={0} | all-to-all | bytes 655360 | tf_op jit(solution)/shard_map/all_to_all | solution.py:477
  134.9 1.1 back0.1
  136.0 17.9 %all_to_all.47 = bf16[128,9,2,128]{3,2,1,0:T(2,128)(2,1)S(1)} all-to-all(bf16[128,9,2,128]{3,2,1,0:T(2,128)(2,1)S(1)} %bitcast.24), channel_id=1, replica_groups=mesh['row'=8,'col'=16] {'row','col'}, dimensions={0} | all-to-all | bytes 1179648 | tf_op jit(solution)/shard_map/all_to_all | solution.py:477
  154.0 1.7 %fifth.1 = f32[48,24,128]{2,1,0:T(8,128)} custom-call(bf16[2304,128]{1,0:T(8,128)(2,1)S(1)} %bitcast.20, f32[1152,128]{1,0:T(8,128)S(1)} %get-tuple-element.74.grad_ref, bf16[1152,128]{1,0:T(8,128)(2,1)S(1)} %get-tuple-element.75.dgate0_ref, f32[1152,128]{1,0:T(8,128)S(1)} %get-tuple-element.76.f0, f32[1152,128]{1,0:T(8,128)S(1)} %get-tuple-element.77.f1, ...), custom_call_target="tpu_custom_call" | custom-call | tf_op jit(solution)/shard_map/fifth/pallas_call | solution.py:462
Async XLA Ops:
  29.2 16.0 %copy-start = (bf16[2,128,640]{2,1,0:T(8,128)(2,1)S(1)}, bf16[2,128,640]{2,1,0:T(8,128)(2,1)}, u32[]{:S(2)}) copy-start(bf16[2,128,640]{2,1,0:T(8,128)(2,1)} %win_ref.7) | copy-start | bytes 983044
  29.2 16.0 %copy-start.1 = (bf16[2,128,128]{2,1,0:T(8,128)(2,1)S(1)}, bf16[2,128,128]{2,1,0:T(8,128)(2,1)}, u32[]{:S(2)}) copy-start(bf16[2,128,128]{2,1,0:T(8,128)(2,1)} %wout_ref.5) | copy-start | bytes 196612
  65.5 16.0 %copy-start.2 = (bf16[48,24,128]{2,1,0:T(8,128)(2,1)S(1)}, bf16[48,24,128]{2,1,0:T(8,128)(2,1)}, u32[]{:S(2)}) copy-start(bf16[48,24,128]{2,1,0:T(8,128)(2,1)} %param.13) | copy-start | bytes 884740

commit v5 on v4

--- a/solution.py
+++ b/solution.py
@@ -374,25 +374,32 @@
         tiles[t * RES:(t + 1) * RES, :] = value[:, t * 128:(t + 1) * 128]
 
 
-def join_two(x_ref, xf, lf, rf, lt, rt):
+def join_two(x_ref, xf, lf, rf, lt, rt, grouped):
     xf[...] = x_ref[...].astype(F32)
     group = COLS * TWO_ROWS
-    for n in range(0, 96, PART):
+    part = 16 if grouped else PART
+    for n in range(0, 96, part):
         def load(r, t):
-            return xf[pl.ds(r * group + 3 * n + t, PART, stride=3), :]
-
-        for p, tiles in swap(load, PART):
-            dst = (lf, rf)[p % 2]
+            return xf[pl.ds(r * group + 3 * n + t, part, stride=3), :]
+
+        for p, tiles in swap(load, part):
             for t in range(3):
-                dst[pl.ds(t * RES + 4 * n + p // 2, PART, stride=4), :] = tiles[t]
-    narrow(lf, lt)
-    narrow(rf, rt)
-
-
-def split_two(lf, rf, o_ref, of):
+                if grouped:
+                    start = p // 2 * 96 + n
+                    (lt, rt)[p % 2][start:start + part, t * 128:(t + 1) * 128] = tiles[t].astype(BF16)
+                else:
+                    (lf, rf)[p % 2][pl.ds(t * RES + 4 * n + p // 2, part, stride=4), :] = tiles[t]
+    if not grouped:
+        narrow(lf, lt)
+        narrow(rf, rt)
+
+
+def split_two(lf, rf, o_ref, of, grouped):
     group = COLS * TWO_ROWS
     for n in range(0, 96, PART):
         def load(p, t):
+            if grouped:
+                return (lf, rf)[p % 2][pl.ds(t * RES + p // 2 * 96 + n, PART), :]
             return (lf, rf)[p % 2][pl.ds(t * RES + 4 * n + p // 2, PART, stride=4), :]
 
         for r, tiles in swap(load, PART):
@@ -429,7 +436,7 @@
 
 
 def m_forward(u, x_ref, o_ref, lt, rt, xf, lf, rf, prod, of):
-    join_two(x_ref, xf, lf, rf, lt, rt)
+    join_two(x_ref, xf, lf, rf, lt, rt, u == 0)
     if u == 0:
         keep(prod, mm_tn(rt[...], lt[...]))
     else:
@@ -445,7 +452,7 @@
     else:
         keep(prod_l, mm_tn(dt[...], rt[...]))
         keep(prod_r, mm(dt[...], lt[...]))
-    split_two(prod_l, prod_r, o_ref, of)
+    split_two(prod_l, prod_r, o_ref, of, u == 0)
 
 
 def shape(*dims, dtype=BF16):

time: 156 us -> 156 us (level)
  no operation moved by 1% of the time
where the time goes in v5:
time: 156 us
  blocking collectives  143 us (92%)
  Pallas kernels  12.1 us (8%)
    all_to_all x8, blocking collectives, exchange(): lax.all_to_all(message, AXES, 0, 0, tiled=True)  143 us
    pallas_call x9, Pallas kernels, run(): pl.pallas_call(fn, out_shape=outs, in_specs=specs, out_specs=[HB if k in...  12.1 us

profile of v5, /device:TPU:1, one launch (start us, length us, event | category | flops | bytes accessed | tf_op | source)
XLA Modules:
  0.0 155.8 jit_solution(15994643040454829583)
XLA Ops:
  0.6 2.0 %first.1 = (bf16[2304,128]{1,0:T(8,128)(2,1)S(1)}, bf16[1152,128]{1,0:T(8,128)(2,1)S(1)}, f32[1152,128]{1,0:T(8,128)S(1)}, f32[2,128]{1,0:T(2,128)S(1)}, f32[2,1...) custom-call(s32[3,3]{1,0:T(4,128)} %far_mask_ref.1, ...), custom_call_target="tpu_custom_call" | custom-call | tf_op jit(solution)/shard_map/first/pallas_call | solution.py:469
  2.6 25.5 %all_to_all.40 = bf16[128,9,2,128]{3,2,1,0:T(2,128)(2,1)S(1)} all-to-all(bf16[128,9,2,128]{3,2,1,0:T(2,128)(2,1)S(1)} %bitcast.30), channel_id=1, replica_groups=mesh['row'=8,'col'=16] {'row','col'}, dimensions={0} | all-to-all | bytes 1179648 | tf_op jit(solution)/shard_map/all_to_all | solution.py:484
  28.1 1.0 product0.1
  29.1 0.0 copy-start
  29.1 0.0 copy-start.1
  29.1 16.0 %all_to_all.41 = bf16[128,5,2,128]{3,2,1,0:T(2,128)(2,1)S(1)} all-to-all(bf16[128,5,2,128]{3,2,1,0:T(2,128)(2,1)S(1)} %bitcast.33), channel_id=1, replica_groups=mesh['row'=8,'col'=16] {'row','col'}, dimensions={0} | all-to-all | bytes 655360 | tf_op jit(solution)/shard_map/all_to_all | solution.py:484
  45.1 0.0 copy-done
  45.1 0.0 copy-done.1
  45.1 1.4 second.1
  46.5 17.9 %all_to_all.42 = bf16[128,9,2,128]{3,2,1,0:T(2,128)(2,1)S(1)} all-to-all(bf16[128,9,2,128]{3,2,1,0:T(2,128)(2,1)S(1)} %bitcast.29), channel_id=1, replica_groups=mesh['row'=8,'col'=16] {'row','col'}, dimensions={0} | all-to-all | bytes 1179648 | tf_op jit(solution)/shard_map/all_to_all | solution.py:484
  64.5 0.9 product1.1
  65.4 0.0 copy-start.2
  65.4 16.0 %all_to_all.43 = bf16[128,5,2,128]{3,2,1,0:T(2,128)(2,1)S(1)} all-to-all(bf16[128,5,2,128]{3,2,1,0:T(2,128)(2,1)S(1)} %bitcast.34), channel_id=1, replica_groups=mesh['row'=8,'col'=16] {'row','col'}, dimensions={0} | all-to-all | bytes 655360 | tf_op jit(solution)/shard_map/all_to_all | solution.py:484
  81.4 0.0 copy-done.2
  81.4 1.2 third.1
  82.6 15.5 %all_to_all.44 = bf16[128,5,2,128]{3,2,1,0:T(2,128)(2,1)S(1)} all-to-all(bf16[128,5,2,128]{3,2,1,0:T(2,128)(2,1)S(1)} %bitcast.32), channel_id=1, replica_groups=mesh['row'=8,'col'=16] {'row','col'}, dimensions={0} | all-to-all | bytes 655360 | tf_op jit(solution)/shard_map/all_to_all | solution.py:484
  98.1 1.1 back1.1
  99.3 17.9 %all_to_all.45 = bf16[128,9,2,128]{3,2,1,0:T(2,128)(2,1)S(1)} all-to-all(bf16[128,9,2,128]{3,2,1,0:T(2,128)(2,1)S(1)} %bitcast.23), channel_id=1, replica_groups=mesh['row'=8,'col'=16] {'row','col'}, dimensions={0} | all-to-all | bytes 1179648 | tf_op jit(solution)/shard_map/all_to_all | solution.py:484
  117.2 1.6 %fourth.1 = (bf16[1280,128]{1,0:T(8,128)(2,1)S(1)}, f32[1152,128]{1,0:T(8,128)S(1)}, bf16[1152,128]{1,0:T(8,128)(2,1)S(1)}, bf16[1152,128]{1,0:T(8,128)(2,1)}) custom-call(bf16[2304,128]{1,0:T(8,128)(2,1)S(1)} %bitcast.19, bf16[1152,128]{1,0:T(8,128)(2,1)S(1)} %get-tuple-element.58.cot_ref, bf16[1152,128]{1,0:T(8,128)(2,1)S(1)} %get-tuple-element.59.dgate1_ref, ...), custom_call_target="tpu_custom_call" | custom-call | tf_op jit(solution)/shard_map/fourth/pallas_call | solution.py:469
  118.9 16.0 %all_to_all.46 = bf16[128,5,2,128]{3,2,1,0:T(2,128)(2,1)S(1)} all-to-all(bf16[128,5,2,128]{3,2,1,0:T(2,128)(2,1)S(1)} %bitcast.31), channel_id=1, replica_groups=mesh['row'=8,'col'=16] {'row','col'}, dimensions={0} | all-to-all | bytes 655360 | tf_op jit(solution)/shard_map/all_to_all | solution.py:484
  134.9 1.1 back0.1
  136.0 17.9 %all_to_all.47 = bf16[128,9,2,128]{3,2,1,0:T(2,128)(2,1)S(1)} all-to-all(bf16[128,9,2,128]{3,2,1,0:T(2,128)(2,1)S(1)} %bitcast.24), channel_id=1, replica_groups=mesh['row'=8,'col'=16] {'row','col'}, dimensions={0} | all-to-all | bytes 1179648 | tf_op jit(solution)/shard_map/all_to_all | solution.py:484
  154.0 1.7 %fifth.1 = f32[48,24,128]{2,1,0:T(8,128)} custom-call(bf16[2304,128]{1,0:T(8,128)(2,1)S(1)} %bitcast.20, f32[1152,128]{1,0:T(8,128)S(1)} %get-tuple-element.74.grad_ref, bf16[1152,128]{1,0:T(8,128)(2,1)S(1)} %get-tuple-element.75.dgate0_ref, f32[1152,128]{1,0:T(8,128)S(1)} %get-tuple-element.76.f0, f32[1152,128]{1,0:T(8,128)S(1)} %get-tuple-element.77.f1, ...), custom_call_target="tpu_custom_call" | custom-call | tf_op jit(solution)/shard_map/fifth/pallas_call | solution.py:469
Async XLA Ops:
  29.1 16.0 %copy-start = (bf16[2,128,640]{2,1,0:T(8,128)(2,1)S(1)}, bf16[2,128,640]{2,1,0:T(8,128)(2,1)}, u32[]{:S(2)}) copy-start(bf16[2,128,640]{2,1,0:T(8,128)(2,1)} %win_ref.7) | copy-start | bytes 983044
  29.1 16.0 %copy-start.1 = (bf16[2,128,128]{2,1,0:T(8,128)(2,1)S(1)}, bf16[2,128,128]{2,1,0:T(8,128)(2,1)}, u32[]{:S(2)}) copy-start(bf16[2,128,128]{2,1,0:T(8,128)(2,1)} %wout_ref.5) | copy-start | bytes 196612
  65.4 16.0 %copy-start.2 = (bf16[48,24,128]{2,1,0:T(8,128)(2,1)S(1)}, bf16[48,24,128]{2,1,0:T(8,128)(2,1)}, u32[]{:S(2)}) copy-start(bf16[48,24,128]{2,1,0:T(8,128)(2,1)} %param.13) | copy-start | bytes 884740
